TPU v7x, 256 devices: a whole 4x4x8 slice. The times are simulated.
256 devices in a mesh: seq: 64 (over y, x_hi, z), head: 4 (over x_lo, core).
Axes of the slice: x: 4 (x_hi: 2, x_lo: 2; x = x_hi * 2 + x_lo), y: 4, z: 8, core: 2. Of those that a mesh axis runs over, the one named last changes fastest.
Arguments:
- qkv: bfloat16 [3, 49152, 1536], P(None, ('seq', 'head')), may hold values from -5 to 5
- key_tiles: int32 [12, 128, 27], P('head', 'seq'), may hold values from -1 to 127, as said below
Outputs:
- attended: bfloat16 [49152, 1536], P(('seq', 'head'))
Inputs may be any that keep to these rules, and one draw needn't show every extreme that they name: Each list key_tiles[n, g] names distinct tiles, the query tile g among them, each differing from g by at most 1 in the time tile, the tile row and the tile column; named tiles come first and -1 fills the rest of the list.
All inputs are finite; a program needn't handle non-finite values.
Results may differ from a plain program's by a relative error of at most 0.0035.
Values may be sent and summed in bfloat16 or wider, within the bound.
No kernel may reach another device: no remote copies, remote signals or barrier semaphores. Data moves between devices by JAX's collectives and lax.ppermute only.
A program may use at most 192 MiB of HBM per device.

v0:
```python
import functools
import math

import jax
import jax.numpy as jnp
from jax import lax
from jax.experimental import pallas as pl
from jax.experimental.pallas import tpu as pltpu
from jax.sharding import PartitionSpec as P

TIME_TILES = 4
AXES = ("seq", "head")
FAR = -1e30
VMEM_LIMIT = 28 * 2**20
VMEM_SMALL = 12 * 2**20
BATCH = 2
EXTRA = 16
POOL = 9


def linear(y, xh, z, xl, core):
    return ((y * 2 + xh) * 8 + z) * 4 + xl * 2 + core


def devices():
    for y in range(4):
        for xh in range(2):
            for z in range(8):
                for xl in range(2):
                    for core in range(2):
                        yield y, xh, z, xl, core


def spread_pairs(k):
    pairs = []
    for y, xh, z, xl, core in devices():
        group = (2 * xl + core) ^ k
        pairs.append((linear(y, xh, z, xl, core), linear(y, group >> 1, z, group & 1, xh)))
    return pairs


def gather_pairs(k):
    return [(b, a) for a, b in spread_pairs(k)]


def edge_pairs():
    return [(linear(y, xh, z, xl, c), linear(y, xh, z ^ 4, xl, c)) for y, xh, z, xl, c in devices()]


def core_pairs():
    return [(linear(y, xh, z, xl, c), linear(y, xh, z, xl, 1 - c)) for y, xh, z, xl, c in devices()]


def column_pairs():
    pairs = []
    for y, xh, z, xl, core in devices():
        to = y + (1 if core == 1 else -1)
        if 0 <= to < 4:
            pairs.append((linear(y, xh, z, xl, core), linear(to, xh, z, xl, 1 - core)))
    return pairs


def time_pairs(by):
    pairs = []
    for y, xh, z, xl, core in devices():
        if 0 <= z % TIME_TILES + by < TIME_TILES:
            pairs.append((linear(y, xh, z, xl, core), linear(y, xh, z + by, xl, core)))
    return pairs


def send(x, pairs):
    return lax.ppermute(x, AXES, pairs)


def split_kernel(at_ref, qkv_ref, names_ref, *outs):
    width = outs[0].shape[-1]
    rows = qkv_ref.shape[1]
    for k in range(4):
        lanes = pl.ds(pl.multiple_of((at_ref[0] ^ k) * width, 128), width)
        outs[k][:rows, :] = qkv_ref[0, :, lanes]
        outs[k][rows:, :] = names_ref[...]
        outs[4 + k][...] = qkv_ref[1:3, :, lanes]


def split(at, qkv, names):
    _, rows, columns = qkv.shape
    width = columns // 4
    vmem = pl.BlockSpec(memory_space=pltpu.VMEM)
    shapes = [jax.ShapeDtypeStruct((rows + EXTRA, width), qkv.dtype)] * 4
    shapes += [jax.ShapeDtypeStruct((2, rows, width), qkv.dtype)] * 4
    return pl.pallas_call(
        split_kernel,
        out_shape=shapes,
        in_specs=[pl.BlockSpec(memory_space=pltpu.SMEM), vmem, vmem],
        out_specs=[vmem] * 8,
        compiler_params=pltpu.CompilerParams(vmem_limit_bytes=VMEM_SMALL),
        name="split",
    )(at, qkv, names)


def stack_kernel(place_ref, *refs):
    parts, kv_ref, edge_ref, sems = refs[:4], refs[4], refs[5], refs[6]
    rows = parts[0].shape[1]
    copies = []
    for k in range(4):
        copies.append(pltpu.make_async_copy(parts[k], kv_ref.at[:, pl.ds(k * rows, rows)], sems.at[k]))
    for copy in copies:
        copy.start()
    for copy in copies:
        copy.wait()
    edge_ref[...] = kv_ref[:, pl.ds(pl.multiple_of(place_ref[0] * (2 * rows), 128), 2 * rows), :]


def stack(place, parts):
    _, rows, width = parts[0].shape
    vmem = pl.BlockSpec(memory_space=pltpu.VMEM)
    return pl.pallas_call(
        stack_kernel,
        out_shape=[
            jax.ShapeDtypeStruct((2, 4 * rows, width), parts[0].dtype),
            jax.ShapeDtypeStruct((2, 2 * rows, width), parts[0].dtype),
        ],
        in_specs=[pl.BlockSpec(memory_space=pltpu.SMEM)] + [pl.BlockSpec(memory_space=pl.ANY)] * 4,
        out_specs=[vmem] * 2,
        scratch_shapes=[pltpu.SemaphoreType.DMA((4,))],
        compiler_params=pltpu.CompilerParams(vmem_limit_bytes=VMEM_SMALL),
        name="stack",
    )(place, *parts)


def stack_queries_kernel(*refs):
    parts, q_ref, sems = refs[:4], refs[4], refs[5]
    rows = parts[0].shape[0] - EXTRA
    copies = []
    for k in range(4):
        into = q_ref.at[pl.ds(k * rows, rows)]
        copies.append(pltpu.make_async_copy(parts[k].at[pl.ds(0, rows)], into, sems.at[k]))
    into = q_ref.at[pl.ds(4 * rows, EXTRA)]
    copies.append(pltpu.make_async_copy(parts[0].at[pl.ds(rows, EXTRA)], into, sems.at[4]))
    for copy in copies:
        copy.start()
    for copy in copies:
        copy.wait()


def stack_queries(parts):
    rows, width = parts[0].shape[0] - EXTRA, parts[0].shape[1]
    return pl.pallas_call(
        stack_queries_kernel,
        out_shape=jax.ShapeDtypeStruct((4 * rows + EXTRA, width), parts[0].dtype),
        in_specs=[pl.BlockSpec(memory_space=pl.ANY)] * 4,
        out_specs=pl.BlockSpec(memory_space=pltpu.VMEM),
        scratch_shapes=[pltpu.SemaphoreType.DMA((5,))],
        compiler_params=pltpu.CompilerParams(vmem_limit_bytes=VMEM_SMALL),
        name="stack_queries",
    )(*parts)


def join_kernel(at_ref, *refs):
    parts, out_ref = refs[:4], refs[4]
    width = parts[0].shape[-1]
    for k in range(4):
        out_ref[:, pl.ds(pl.multiple_of((at_ref[0] ^ k) * width, 128), width)] = parts[k][...]


def join(at, parts):
    rows, width = parts[0].shape
    vmem = pl.BlockSpec(memory_space=pltpu.VMEM)
    return pl.pallas_call(
        join_kernel,
        out_shape=jax.ShapeDtypeStruct((rows, 4 * width), parts[0].dtype),
        in_specs=[pl.BlockSpec(memory_space=pltpu.SMEM)] + [vmem] * 4,
        out_specs=vmem,
        compiler_params=pltpu.CompilerParams(vmem_limit_bytes=VMEM_SMALL),
        name="join",
    )(at, *parts)


def attend_kernel(mask_ref, *refs, sets, pieces, begun, tiles, first_set, first_tile, heads, tile, dim):
    queries = refs[:sets]
    sources = refs[sets : sets + pieces]
    starts = refs[sets + pieces : sets + pieces + begun]
    refs = refs[sets + pieces + begun :]
    outs = refs[:sets]
    pool, held, turned_q, turned_v, max_ref, sum_ref, acc_ref, of_query, of_key = refs[sets : sets + 9]
    rest = refs[sets + 9 :]
    score_refs = (rest[:BATCH], rest[BATCH : 2 * BATCH])
    top_refs = (rest[2 * BATCH : 3 * BATCH], rest[3 * BATCH : 4 * BATCH])
    sems = rest[4 * BATCH]
    count_q = sets * heads * 2

    copies = []
    for n in range(sets):
        copies.append(pltpu.make_async_copy(queries[n].at[pl.ds(0, 2 * tile)], held.at[n], sems.at[n]))
    at = 0
    for source in sources:
        for r in range(source.shape[1] // tile):
            copies.append(
                pltpu.make_async_copy(source.at[:, pl.ds(r * tile, tile)], pool.at[at], sems.at[sets + at])
            )
            at += 1
    for copy in copies:
        copy.start()

    def list_pairs_of(s, count):
        for j in range(tiles):
            of_query[count] = s
            of_key[count] = j
            count = count + mask_ref[(first_set * heads * 2 + s) * POOL + first_tile + j]
        return count

    count = lax.fori_loop(0, count_q, list_pairs_of, 0)
    for i in range(4 * BATCH):
        of_query[count + i] = count_q
        of_key[count + i] = 0
    scale = dim**-0.5
    factor = scale * math.log2(math.e)
    width = heads * dim
    if begun:
        sum_ref[...] = jnp.full_like(sum_ref, 0.125)
        for n in range(sets):
            for h in range(heads):
                lse = starts[n][width + 3 * h : width + 3 * h + 1, :]
                for i in range(1, 3):
                    lse = lse + starts[n][width + 3 * h + i : width + 3 * h + i + 1, :]
                for p in range(2):
                    s = (n * heads + h) * 2 + p
                    at = slice(p * tile, (p + 1) * tile)
                    max_ref[s, :1, :] = lse[:, at] / scale
                    acc_ref[s] = starts[n][h * dim : (h + 1) * dim, at]
        max_ref[count_q] = jnp.zeros((8, tile), jnp.float32)
        acc_ref[count_q] = jnp.zeros((dim, tile), jnp.float32)
    else:
        max_ref[...] = jnp.full_like(max_ref, FAR)
        sum_ref[...] = jnp.zeros_like(sum_ref)
        acc_ref[...] = jnp.zeros_like(acc_ref)
    for copy in copies:
        copy.wait()
    for n in range(sets):
        for h in range(heads):
            for p in range(2):
                turned_q[(n * heads + h) * 2 + p] = jnp.transpose(
                    held[n, p * tile : (p + 1) * tile, h * dim : (h + 1) * dim]
                )
    turned_q[count_q] = turned_q[0]
    for h in range(heads):
        for j in range(tiles):
            turned_v[h * tiles + j] = jnp.transpose(pool[j, 1, :, h * dim : (h + 1) * dim])

    def score(i, out_ref, top_ref):
        s, j = of_query[i], of_key[i]
        h = lax.rem(s // 2, heads)
        keys = pool[j, 0, :, pl.ds(pl.multiple_of(h * dim, dim), dim)]
        scores = jnp.dot(keys, turned_q[s], preferred_element_type=jnp.float32)
        out_ref[...] = scores
        top_ref[...] = jnp.max(scores.reshape(tile // 8, 8, tile), axis=0)

    def weigh(i, in_ref, top_ref):
        s, j = of_query[i], of_key[i]
        h = lax.rem(s // 2, heads)
        old = max_ref[s, :1, :]
        new = jnp.maximum(old, jnp.max(top_ref[...], axis=0, keepdims=True))
        shrink = jnp.exp2((old - new) * factor)
        max_ref[s, :1, :] = new
        weights = jnp.exp2((in_ref[...] - new) * factor)
        sum_ref[s] = sum_ref[s] * shrink + jnp.sum(weights.reshape(tile // 8, 8, tile), axis=0)
        acc_ref[s] = acc_ref[s] * shrink + jnp.dot(
            turned_v[h * tiles + j], weights.astype(jnp.bfloat16), preferred_element_type=jnp.float32
        )

    for u in range(BATCH):
        score(u, score_refs[0][u], top_refs[0][u])

    def step(t, carry):
        for half in range(2):
            base = (2 * t + half) * BATCH
            for u in range(BATCH):
                score(base + BATCH + u, score_refs[1 - half][u], top_refs[1 - half][u])
            for u in range(BATCH):
                weigh(base + u, score_refs[half][u], top_refs[half][u])
        return carry

    lax.fori_loop(0, (count + 2 * BATCH - 1) // (2 * BATCH), step, 0)

    for n in range(sets):
        outs[n][width : width + EXTRA, :] = jnp.zeros((EXTRA, 2 * tile), outs[n].dtype)
        for h in range(heads):
            for p in range(2):
                s = (n * heads + h) * 2 + p
                at = slice(p * tile, (p + 1) * tile)
                total = jnp.maximum(jnp.sum(sum_ref[s], axis=0, keepdims=True), 1e-30)
                outs[n][h * dim : (h + 1) * dim, at] = (acc_ref[s] / total).astype(outs[n].dtype)
                left = max_ref[s, :1, :] * scale + jnp.log(total)
                for i in range(3):
                    part = left.astype(outs[n].dtype)
                    outs[n][width + 3 * h + i : width + 3 * h + i + 1, at] = part
                    left = left - part.astype(jnp.float32)


def attend(mask, queries, sources, starts, heads, first_set, first_tile, out_dtype):
    sets = len(queries)
    brick, width = queries[0].shape[0] - EXTRA, queries[0].shape[1]
    tile = brick // 2
    dim = width // heads
    tiles = sum(source.shape[1] for source in sources) // tile
    count_q = sets * heads * 2
    hbm = pl.BlockSpec(memory_space=pl.ANY)
    vmem = pl.BlockSpec(memory_space=pltpu.VMEM)
    return pl.pallas_call(
        functools.partial(
            attend_kernel,
            sets=sets,
            pieces=len(sources),
            begun=len(starts),
            tiles=tiles,
            first_set=first_set,
            first_tile=first_tile,
            heads=heads,
            tile=tile,
            dim=dim,
        ),
        out_shape=[jax.ShapeDtypeStruct((width + EXTRA, brick), out_dtype)] * sets,
        in_specs=[pl.BlockSpec(memory_space=pltpu.SMEM)] + [hbm] * (sets + len(sources)) + [vmem] * len(starts),
        out_specs=[vmem] * sets,
        scratch_shapes=[
            pltpu.VMEM((tiles, 2, tile, width), jnp.bfloat16),
            pltpu.VMEM((sets, brick, width), jnp.bfloat16),
            pltpu.VMEM((count_q + 1, dim, tile), jnp.bfloat16),
            pltpu.VMEM((tiles * heads, dim, tile), jnp.bfloat16),
            pltpu.VMEM((count_q + 1, 8, tile), jnp.float32),
            pltpu.VMEM((count_q + 1, 8, tile), jnp.float32),
            pltpu.VMEM((count_q + 1, dim, tile), jnp.float32),
            pltpu.SMEM((count_q * tiles + 8 * BATCH,), jnp.int32),
            pltpu.SMEM((count_q * tiles + 8 * BATCH,), jnp.int32),
        ]
        + [pltpu.VMEM((tile, tile), jnp.float32)] * (2 * BATCH)
        + [pltpu.VMEM((8, tile), jnp.float32)] * (2 * BATCH)
        + [pltpu.SemaphoreType.DMA((sets + tiles,))],
        compiler_params=pltpu.CompilerParams(vmem_limit_bytes=VMEM_LIMIT),
        name=f"attend_{sets}_{tiles}",
    )(mask, *queries, *sources, *starts)


def merge_kernel(valid_ref, *refs, heads):
    parts, outs = refs[:3], refs[3:]
    width, brick = parts[0].shape[0] - EXTRA, parts[0].shape[1]
    dim = width // heads
    quarter = brick // 4
    for h in range(heads):
        lse = []
        for i in range(3):
            rows = parts[i][width : width + EXTRA, :].astype(jnp.float32)
            lse.append(rows[3 * h : 3 * h + 1] + rows[3 * h + 1 : 3 * h + 2] + rows[3 * h + 2 : 3 * h + 3])
        lse[1] = jnp.where(valid_ref[0] > 0, lse[1], FAR)
        lse[2] = jnp.where(valid_ref[1] > 0, lse[2], FAR)
        top = jnp.maximum(jnp.maximum(lse[0], lse[1]), lse[2])
        shares = [jnp.exp(x - top) for x in lse]
        total = shares[0] + shares[1] + shares[2]
        lanes = slice(h * dim, (h + 1) * dim)
        merged = parts[0][lanes, :].astype(jnp.float32) * (shares[0] / total)
        merged += parts[1][lanes, :].astype(jnp.float32) * (shares[1] / total)
        merged += parts[2][lanes, :].astype(jnp.float32) * (shares[2] / total)
        merged = jnp.transpose(merged).astype(jnp.bfloat16)
        for k in range(4):
            outs[k][:, lanes] = merged[k * quarter : (k + 1) * quarter, :]


def merge(valid, parts, heads):
    width, brick = parts[0].shape[0] - EXTRA, parts[0].shape[1]
    vmem = pl.BlockSpec(memory_space=pltpu.VMEM)
    return pl.pallas_call(
        functools.partial(merge_kernel, heads=heads),
        out_shape=[jax.ShapeDtypeStruct((brick // 4, width), jnp.bfloat16)] * 4,
        in_specs=[pl.BlockSpec(memory_space=pltpu.SMEM)] + [vmem] * 3,
        out_specs=[vmem] * 4,
        compiler_params=pltpu.CompilerParams(vmem_limit_bytes=VMEM_SMALL),
        name="merge",
    )(valid, *parts)


def named(lists, column, pair, time, xh):
    tile_time = lists // 2 % TIME_TILES
    tile_pair = lists // (2 * TIME_TILES) % 2
    tile_column = lists // (4 * TIME_TILES)
    beside = jnp.where(tile_column == column + 1 - 2 * (column % 2), 1, 2)
    column_slot = jnp.where(tile_column == column, 0, beside)
    slot = jnp.where(tile_pair == pair, column_slot * 2 + ((lists % 2) ^ xh), 6 + column_slot)
    slot = jnp.where((lists >= 0) & (tile_time == time), slot, -1)
    mask = jnp.any(slot[..., None] == jnp.arange(POOL, dtype=jnp.int32), axis=-2)
    return jnp.where(xh == 1, mask[..., ::-1, :], mask)


def local(qkv, key_tiles):
    heads = key_tiles.shape[0]
    seq = lax.axis_index("seq")
    head = lax.axis_index("head")
    y, xh, z = seq // 16, seq // 8 % 2, seq % 8
    core = head % 2
    pair, time = z // TIME_TILES, z % TIME_TILES
    at = head.astype(jnp.int32).reshape(1)
    place = ((1 - pair) ^ xh).astype(jnp.int32).reshape(1)
    valid = jnp.stack([time > 0, time < TIME_TILES - 1])

    entries = key_tiles.size
    names = key_tiles.astype(jnp.bfloat16).reshape(1, entries)
    names = jnp.pad(names, ((0, EXTRA - 1), (0, qkv.shape[2] // 4 - entries)))
    pieces = split(at, qkv, names)
    q_parts = [send(pieces[k], spread_pairs(k)) for k in range(4)]
    kv_pieces = list(pieces[4:])
    for k in range(1, 4):
        q_parts[k], kv_pieces[k] = lax.optimization_barrier((q_parts[k], kv_pieces[k]))
    kv_parts = [send(kv_pieces[k], spread_pairs(k)) for k in range(4)]
    q_own = stack_queries(q_parts)
    q_prev = send(q_own, time_pairs(1))
    q_next = send(q_own, time_pairs(-1))
    place, q_prev, q_next = lax.optimization_barrier((place, q_prev, q_next))
    lists = jnp.stack([q[-EXTRA, :entries] for q in (q_own, q_prev, q_next)])
    lists = lists.astype(jnp.int32).reshape((3,) + key_tiles.shape)
    mask = named(lists, 2 * y + core, pair, time, xh)
    here = jnp.concatenate([jnp.ones((1,), bool), valid])
    mask = (mask & here[:, None, None, None]).astype(jnp.int32).reshape(-1)
    kv_own, edge = stack(place, kv_parts)
    edge_own = send(edge, edge_pairs())
    bodies = (kv_own, send(kv_own, core_pairs()), send(kv_own, column_pairs()))

    begun = attend(mask, (q_own, q_prev, q_next), bodies, (), heads, 0, 0, jnp.float32)
    begun, edge_own = lax.optimization_barrier((begun, edge_own))
    edges = (edge_own, send(edge_own, core_pairs()), send(edge_own, column_pairs()))
    o_prev, o_next = attend(mask, (q_prev, q_next), edges, begun[1:], heads, 1, 6, jnp.bfloat16)
    o_before = send(o_next, time_pairs(1))
    o_after = send(o_prev, time_pairs(-1))
    (o_own,) = attend(mask, (q_own,), edges, begun[:1], heads, 0, 6, jnp.float32)

    chunks = merge(valid.astype(jnp.int32), (o_own, o_before, o_after), heads)
    home = [send(chunks[k], gather_pairs(k)) for k in range(4)]
    return join(at, home)


def solution(mesh):
    placed = (P(None, ("seq", "head"), None), P("head", "seq", None))
    return jax.shard_map(
        local, mesh=mesh, in_specs=placed, out_specs=P(("seq", "head"), None), check_vma=False
    )
```

profile of v0, /device:TPU:8, one launch (start us, length us, event | category | flops | bytes accessed | tf_op | source)
XLA Modules:
  0.0 134.7 jit_solution(2640787793333179950)
XLA Ops:
  0.0 0.7 convert_element_type.18
  0.8 1.5 %copy-done = bf16[3,192,1536]{2,1,0:T(8,128)(2,1)S(1)} copy-done((bf16[3,192,1536]{2,1,0:T(8,128)(2,1)S(1)}, bf16[3,192,1536]{2,1,0:T(8,128)(2,1)}, u32[]{:S(2)}) %copy-start) | copy-done | bytes 1769496
  2.3 1.0 split.1
  3.3 1.5 %collective-permute-start.1 = (bf16[208,384]{1,0:T(8,128)(2,1)S(1)}, bf16[208,384]{1,0:T(8,128)(2,1)S(1)}, u32[]{:S(2)}, u32[]{:S(2)}) collective-permute-start(bf16[208,384]{1,0:T(8,128)(2,1)S(1)} %get-tuple-element.38), channel_id=1, source_target_pairs={{0,2},{1,0},{2,34},{3,32},{4,6},{5,4},{6,38},{7,36},{8,10},{9,8},{... | collective-permute-start | bytes 479240 | tf_op jit(solution)/shard_map/ppermute | solution.py:72
  4.7 1.5 %collective-permute-start.2 = (bf16[208,384]{1,0:T(8,128)(2,1)S(1)}, bf16[208,384]{1,0:T(8,128)(2,1)S(1)}, u32[]{:S(2)}, u32[]{:S(2)}) collective-permute-start(bf16[208,384]{1,0:T(8,128)(2,1)S(1)} %get-tuple-element.41), channel_id=1, source_target_pairs={{0,32},{1,34},{2,0},{3,2},{4,36},{5,38},{6,4},{7,6},{8,40},{9,42},... | collective-permute-start | bytes 479240 | tf_op jit(solution)/shard_map/ppermute | solution.py:72
  6.3 2.2 %collective-permute-start.3 = (bf16[208,384]{1,0:T(8,128)(2,1)S(1)}, bf16[208,384]{1,0:T(8,128)(2,1)S(1)}, u32[]{:S(2)}, u32[]{:S(2)}) collective-permute-start(bf16[208,384]{1,0:T(8,128)(2,1)S(1)} %get-tuple-element.44), channel_id=1, source_target_pairs={{0,34},{1,32},{2,2},{3,0},{4,38},{5,36},{6,6},{7,4},{8,42},{9,40},... | collective-permute-start | bytes 479240 | tf_op jit(solution)/shard_map/ppermute | solution.py:72
  8.5 0.7 collective-permute-start
  9.2 3.3 %collective-permute-done.2.refs_2_ = bf16[208,384]{1,0:T(8,128)(2,1)S(1)} collective-permute-done((bf16[208,384]{1,0:T(8,128)(2,1)S(1)}, bf16[208,384]{1,0:T(8,128)(2,1)S(1)}, u32[]{:S(2)}, u32[]{:S(2)}) %collective-permute-start.2) | collective-permute-done | bytes 159776 | tf_op jit(solution)/shard_map/ppermute | solution.py:72
  12.5 1.1 collective-permute-done.3.refs_3_
  13.6 0.8 stack_queries.1.refs_0_
  14.4 1.3 collective-permute-start.5
  15.7 4.6 %collective-permute-start.4 = (bf16[784,384]{1,0:T(8,128)(2,1)S(1)}, bf16[784,384]{1,0:T(8,128)(2,1)S(1)}, u32[]{:S(2)}, u32[]{:S(2)}) collective-permute-start(bf16[784,384]{1,0:T(8,128)(2,1)S(1)} %stack_queries.1.refs_0_), channel_id=1, source_target_pairs={{0,4},{1,5},{2,6},{3,7},{4,8},{5,9},{6,10},{7,11},{8,12},{9,13},{1... | collective-permute-start | bytes 1806344 | tf_op jit(solution)/shard_map/ppermute | solution.py:72
  20.3 1.6 %collective-permute-start.6 = (bf16[2,192,384]{2,1,0:T(8,128)(2,1)}, bf16[2,192,384]{2,1,0:T(8,128)(2,1)S(1)}, u32[]{:S(2)}, u32[]{:S(2)}) collective-permute-start(bf16[2,192,384]{2,1,0:T(8,128)(2,1)} %get-tuple-element.50), channel_id=1, source_target_pairs={{0,0},{1,2},{2,32},{3,34},{4,4},{5,6},{6,36},{7,38},{8,8},{9,10},{... | collective-permute-start | bytes 884744 | tf_op jit(solution)/shard_map/ppermute | solution.py:72
  21.9 8.3 %collective-permute-start.9 = (bf16[2,192,384]{2,1,0:T(8,128)(2,1)}, bf16[2,192,384]{2,1,0:T(8,128)(2,1)S(1)}, u32[]{:S(2)}, u32[]{:S(2)}) collective-permute-start(bf16[2,192,384]{2,1,0:T(8,128)(2,1)} %get-tuple-element.53), channel_id=1, source_target_pairs={{0,34},{1,32},{2,2},{3,0},{4,38},{5,36},{6,6},{7,4},{8,42},{9,40},... | collective-permute-start | bytes 884744 | tf_op jit(solution)/shard_map/ppermute | solution.py:72
  30.3 0.1 collective-permute-done.5.refs_2_.refs_1_
  30.4 5.1 %collective-permute-start.7 = (bf16[2,192,384]{2,1,0:T(8,128)(2,1)S(1)}, bf16[2,192,384]{2,1,0:T(8,128)(2,1)S(1)}, u32[]{:S(2)}, u32[]{:S(2)}) collective-permute-start(bf16[2,192,384]{2,1,0:T(8,128)(2,1)S(1)} %get-tuple-element.51), channel_id=1, source_target_pairs={{0,2},{1,0},{2,34},{3,32},{4,6},{5,4},{6,38},{7,36},{8,10},{9,8},{... | collective-permute-start | bytes 884744 | tf_op jit(solution)/shard_map/ppermute | solution.py:72
  35.5 3.6 %collective-permute-done.9.refs_3_ = bf16[2,192,384]{2,1,0:T(8,128)(2,1)S(1)} collective-permute-done((bf16[2,192,384]{2,1,0:T(8,128)(2,1)}, bf16[2,192,384]{2,1,0:T(8,128)(2,1)S(1)}, u32[]{:S(2)}, u32[]{:S(2)}) %collective-permute-start.9) | collective-permute-done | bytes 294944 | tf_op jit(solution)/shard_map/ppermute | solution.py:72
  39.1 0.7 collective-permute-done.8.refs_2_
  39.8 0.4 collective-permute-done.7.refs_1_
  40.2 1.2 stack.26
  41.4 0.8 copy-done.1
  42.2 4.0 %collective-permute-start.11 = (bf16[2,768,384]{2,1,0:T(8,128)(2,1)}, bf16[2,768,384]{2,1,0:T(8,128)(2,1)}, u32[]{:S(2)}, u32[]{:S(2)}) collective-permute-start(bf16[2,768,384]{2,1,0:T(8,128)(2,1)} %get-tuple-element.54.refs_3_), channel_id=1, source_target_pairs={{1,64},{3,66},{5,68},{7,70},{9,72},{11,74},{13,76},{15,78},{17,80}... | collective-permute-start | bytes 3538952 | tf_op jit(solution)/shard_map/ppermute | solution.py:72
  46.5 7.0 %collective-permute-start.12 = (bf16[2,384,384]{2,1,0:T(8,128)(2,1)}, bf16[2,384,384]{2,1,0:T(8,128)(2,1)S(1)}, u32[]{:S(2)}, u32[]{:S(2)}) collective-permute-start(bf16[2,384,384]{2,1,0:T(8,128)(2,1)} %copy-done.1), channel_id=1, source_target_pairs={{0,16},{1,17},{2,18},{3,19},{4,20},{5,21},{6,22},{7,23},{8,24},{9,... | collective-permute-start | bytes 1769480 | tf_op jit(solution)/shard_map/ppermute | solution.py:72
  53.9 0.1 fusion.2
  54.0 1.0 fusion
  55.0 0.1 copy.7
  55.2 0.1 reshape.132.mask_ref
  55.3 5.1 %collective-permute-done.11.refs_5_ = bf16[2,768,384]{2,1,0:T(8,128)(2,1)} collective-permute-done((bf16[2,768,384]{2,1,0:T(8,128)(2,1)}, bf16[2,768,384]{2,1,0:T(8,128)(2,1)}, u32[]{:S(2)}, u32[]{:S(2)}) %collective-permute-start.11) | collective-permute-done | bytes 1179680 | tf_op jit(solution)/shard_map/ppermute | solution.py:72
  60.5 11.8 %attend_3_6.1 = (f32[400,768]{1,0:T(8,128)S(1)}, f32[400,768]{1,0:T(8,128)S(1)}, f32[400,768]{1,0:T(8,128)S(1)}) custom-call(s32[162]{0:T(256)S(1)} %reshape.132.mask_ref, bf16[784,384]{1,0:T(8,128)(2,1)S(1)} %stack_queries.1.refs_0_, bf16[784,384]{1,0:T(8,128)(2,1)S(1)} %collective-permute-done.4.refs_1_.refs_0_, ...), custom_call_target="tpu_custom_call" | custom-call | tf_op jit(solution)/shard_map/attend_3_6/pallas_call | solution.py:309
  72.3 6.8 %collective-permute-done.12.refs_1_.refs_2_ = bf16[2,384,384]{2,1,0:T(8,128)(2,1)S(1)} collective-permute-done((bf16[2,384,384]{2,1,0:T(8,128)(2,1)}, bf16[2,384,384]{2,1,0:T(8,128)(2,1)S(1)}, u32[]{:S(2)}, u32[]{:S(2)}) %collective-permute-start.12) | collective-permute-done | bytes 589856 | tf_op jit(solution)/shard_map/ppermute | solution.py:72
  79.1 1.9 %collective-permute-start.14 = (bf16[2,384,384]{2,1,0:T(8,128)(2,1)S(1)}, bf16[2,384,384]{2,1,0:T(8,128)(2,1)S(1)}, u32[]{:S(2)}, u32[]{:S(2)}) collective-permute-start(bf16[2,384,384]{2,1,0:T(8,128)(2,1)S(1)} %collective-permute-done.12.refs_1_.refs_2_), channel_id=1, source_target_pairs={{1,64},{3,66},{5,68},{7,70},{9,72},{11,74},{13,76},{15,78},{17,80}... | collective-permute-start | bytes 1769480 | tf_op jit(solution)/shard_map/ppermute | solution.py:72
  81.0 1.8 %collective-permute-start.13 = (bf16[2,384,384]{2,1,0:T(8,128)(2,1)S(1)}, bf16[2,384,384]{2,1,0:T(8,128)(2,1)S(1)}, u32[]{:S(2)}, u32[]{:S(2)}) collective-permute-start(bf16[2,384,384]{2,1,0:T(8,128)(2,1)S(1)} %collective-permute-done.12.refs_1_.refs_2_), channel_id=1, source_target_pairs={{0,1},{1,0},{2,3},{3,2},{4,5},{5,4},{6,7},{7,6},{8,9},{9,8},{10,11... | collective-permute-start | bytes 1769480 | tf_op jit(solution)/shard_map/ppermute | solution.py:72
  82.8 7.5 %collective-permute-done.14.refs_3_.refs_4_ = bf16[2,384,384]{2,1,0:T(8,128)(2,1)S(1)} collective-permute-done((bf16[2,384,384]{2,1,0:T(8,128)(2,1)S(1)}, bf16[2,384,384]{2,1,0:T(8,128)(2,1)S(1)}, u32[]{:S(2)}, u32[]{:S(2)}) %collective-permute-start.14) | collective-permute-done | bytes 589856 | tf_op jit(solution)/shard_map/ppermute | solution.py:72
  90.3 3.7 %attend_2_3.1 = (bf16[400,768]{1,0:T(8,128)(2,1)S(1)}, bf16[400,768]{1,0:T(8,128)(2,1)S(1)}) custom-call(s32[162]{0:T(256)S(1)} %reshape.132.mask_ref, bf16[784,384]{1,0:T(8,128)(2,1)S(1)} %collective-permute-done.4.refs_1_.refs_0_, bf16[784,384]{1,0:T(8,128)(2,1)S(1)} %collective-permute-done.5.refs_2_.refs_1_, ...), custom_call_target="tpu_custom_call" | custom-call | tf_op jit(solution)/shard_map/attend_2_3/pallas_call | solution.py:309
  94.0 5.0 %collective-permute-start.15 = (bf16[400,768]{1,0:T(8,128)(2,1)S(1)}, bf16[400,768]{1,0:T(8,128)(2,1)S(1)}, u32[]{:S(2)}, u32[]{:S(2)}) collective-permute-start(bf16[400,768]{1,0:T(8,128)(2,1)S(1)} %get-tuple-element.63), channel_id=1, source_target_pairs={{0,4},{1,5},{2,6},{3,7},{4,8},{5,9},{6,10},{7,11},{8,12},{9,13},{1... | collective-permute-start | bytes 1843208 | tf_op jit(solution)/shard_map/ppermute | solution.py:72
  99.0 1.3 collective-permute-start.16
  100.4 2.9 %attend_1_3.1.refs_0_ = f32[400,768]{1,0:T(8,128)S(1)} custom-call(s32[162]{0:T(256)S(1)} %reshape.132.mask_ref, bf16[784,384]{1,0:T(8,128)(2,1)S(1)} %stack_queries.1.refs_0_, bf16[2,384,384]{2,1,0:T(8,128)(2,1)S(1)} %collective-permute-done.12.refs_1_.refs_2_, bf16[2,384,384]{2,1,0:T(8,128)(2,1)S(1)} %collective-permute-done.13.refs_2_.refs_3_, ...), custom_call_target="tpu_custom_call" | custom-call | tf_op jit(solution)/shard_map/attend_1_3/pallas_call | solution.py:309
  103.3 9.1 %collective-permute-done.15.refs_1_ = bf16[400,768]{1,0:T(8,128)(2,1)S(1)} collective-permute-done((bf16[400,768]{1,0:T(8,128)(2,1)S(1)}, bf16[400,768]{1,0:T(8,128)(2,1)S(1)}, u32[]{:S(2)}, u32[]{:S(2)}) %collective-permute-start.15) | collective-permute-done | bytes 614432 | tf_op jit(solution)/shard_map/ppermute | solution.py:72
  112.3 4.2 %collective-permute-done.16.refs_2_ = bf16[400,768]{1,0:T(8,128)(2,1)S(1)} collective-permute-done((bf16[400,768]{1,0:T(8,128)(2,1)S(1)}, bf16[400,768]{1,0:T(8,128)(2,1)S(1)}, u32[]{:S(2)}, u32[]{:S(2)}) %collective-permute-start.16) | collective-permute-done | bytes 614432 | tf_op jit(solution)/shard_map/ppermute | solution.py:72
  116.5 1.1 merge.1
  117.6 0.7 collective-permute-start.17
  118.2 4.0 %collective-permute-start.18 = (bf16[192,384]{1,0:T(8,128)(2,1)S(1)}, bf16[192,384]{1,0:T(8,128)(2,1)S(1)}, u32[]{:S(2)}, u32[]{:S(2)}) collective-permute-start(bf16[192,384]{1,0:T(8,128)(2,1)S(1)} %get-tuple-element.66), channel_id=1, source_target_pairs={{2,0},{0,1},{34,2},{32,3},{6,4},{4,5},{38,6},{36,7},{10,8},{8,9},{... | collective-permute-start | bytes 442376 | tf_op jit(solution)/shard_map/ppermute | solution.py:72
  122.2 0.7 collective-permute-start.19
  122.9 4.5 %collective-permute-start.20 = (bf16[192,384]{1,0:T(8,128)(2,1)S(1)}, bf16[192,384]{1,0:T(8,128)(2,1)S(1)}, u32[]{:S(2)}, u32[]{:S(2)}) collective-permute-start(bf16[192,384]{1,0:T(8,128)(2,1)S(1)} %get-tuple-element.68), channel_id=1, source_target_pairs={{34,0},{32,1},{2,2},{0,3},{38,4},{36,5},{6,6},{4,7},{42,8},{40,9},... | collective-permute-start | bytes 442376 | tf_op jit(solution)/shard_map/ppermute | solution.py:72
  127.5 0.5 collective-permute-done.18.refs_1_
  128.0 1.3 collective-permute-done.19.refs_2_
  129.3 4.6 %collective-permute-done.20.refs_3_ = bf16[192,384]{1,0:T(8,128)(2,1)S(1)} collective-permute-done((bf16[192,384]{1,0:T(8,128)(2,1)S(1)}, bf16[192,384]{1,0:T(8,128)(2,1)S(1)}, u32[]{:S(2)}, u32[]{:S(2)}) %collective-permute-start.20) | collective-permute-done | bytes 147488 | tf_op jit(solution)/shard_map/ppermute | solution.py:72
  133.9 0.9 join.1
  (23 shorter events, 0.9 us)
Async XLA Ops:
  0.8 1.5 %copy-start = (bf16[3,192,1536]{2,1,0:T(8,128)(2,1)S(1)}, bf16[3,192,1536]{2,1,0:T(8,128)(2,1)}, u32[]{:S(2)}) copy-start(bf16[3,192,1536]{2,1,0:T(8,128)(2,1)} %qkv_ref.1) | copy-start | bytes 5308420
  3.3 5.9 %collective-permute-start.1 = (bf16[208,384]{1,0:T(8,128)(2,1)S(1)}, bf16[208,384]{1,0:T(8,128)(2,1)S(1)}, u32[]{:S(2)}, u32[]{:S(2)}) collective-permute-start(bf16[208,384]{1,0:T(8,128)(2,1)S(1)} %get-tuple-element.38), channel_id=1, source_target_pairs={{0,2},{1,0},{2,34},{3,32},{4,6},{5,4},{6,38},{7,36},{8,10},{9,8},{... | collective-permute-start | bytes 479240 | tf_op jit(solution)/shard_map/ppermute | solution.py:72
  4.7 7.8 %collective-permute-start.2 = (bf16[208,384]{1,0:T(8,128)(2,1)S(1)}, bf16[208,384]{1,0:T(8,128)(2,1)S(1)}, u32[]{:S(2)}, u32[]{:S(2)}) collective-permute-start(bf16[208,384]{1,0:T(8,128)(2,1)S(1)} %get-tuple-element.41), channel_id=1, source_target_pairs={{0,32},{1,34},{2,0},{3,2},{4,36},{5,38},{6,4},{7,6},{8,40},{9,42},... | collective-permute-start | bytes 479240 | tf_op jit(solution)/shard_map/ppermute | solution.py:72
  6.3 7.3 %collective-permute-start.3 = (bf16[208,384]{1,0:T(8,128)(2,1)S(1)}, bf16[208,384]{1,0:T(8,128)(2,1)S(1)}, u32[]{:S(2)}, u32[]{:S(2)}) collective-permute-start(bf16[208,384]{1,0:T(8,128)(2,1)S(1)} %get-tuple-element.44), channel_id=1, source_target_pairs={{0,34},{1,32},{2,2},{3,0},{4,38},{5,36},{6,6},{7,4},{8,42},{9,40},... | collective-permute-start | bytes 479240 | tf_op jit(solution)/shard_map/ppermute | solution.py:72
  8.5 5.1 %collective-permute-start = (bf16[208,384]{1,0:T(8,128)(2,1)S(1)}, bf16[208,384]{1,0:T(8,128)(2,1)S(1)}, u32[]{:S(2)}, u32[]{:S(2)}) collective-permute-start(bf16[208,384]{1,0:T(8,128)(2,1)S(1)} %get-tuple-element.37), channel_id=1, source_target_pairs={{0,0},{1,2},{2,32},{3,34},{4,4},{5,6},{6,36},{7,38},{8,8},{9,10},{... | collective-permute-start | bytes 479240 | tf_op jit(solution)/shard_map/ppermute | solution.py:72
  14.4 16.0 %collective-permute-start.5 = (bf16[784,384]{1,0:T(8,128)(2,1)S(1)}, bf16[784,384]{1,0:T(8,128)(2,1)S(1)}, u32[]{:S(2)}, u32[]{:S(2)}) collective-permute-start(bf16[784,384]{1,0:T(8,128)(2,1)S(1)} %stack_queries.1.refs_0_), channel_id=1, source_target_pairs={{4,0},{5,1},{6,2},{7,3},{8,4},{9,5},{10,6},{11,7},{12,8},{13,9},{1... | collective-permute-start | bytes 1806344 | tf_op jit(solution)/shard_map/ppermute | solution.py:72
  15.7 19.8 %collective-permute-start.4 = (bf16[784,384]{1,0:T(8,128)(2,1)S(1)}, bf16[784,384]{1,0:T(8,128)(2,1)S(1)}, u32[]{:S(2)}, u32[]{:S(2)}) collective-permute-start(bf16[784,384]{1,0:T(8,128)(2,1)S(1)} %stack_queries.1.refs_0_), channel_id=1, source_target_pairs={{0,4},{1,5},{2,6},{3,7},{4,8},{5,9},{6,10},{7,11},{8,12},{9,13},{1... | collective-permute-start | bytes 1806344 | tf_op jit(solution)/shard_map/ppermute | solution.py:72
  20.3 15.2 %collective-permute-start.6 = (bf16[2,192,384]{2,1,0:T(8,128)(2,1)}, bf16[2,192,384]{2,1,0:T(8,128)(2,1)S(1)}, u32[]{:S(2)}, u32[]{:S(2)}) collective-permute-start(bf16[2,192,384]{2,1,0:T(8,128)(2,1)} %get-tuple-element.50), channel_id=1, source_target_pairs={{0,0},{1,2},{2,32},{3,34},{4,4},{5,6},{6,36},{7,38},{8,8},{9,10},{... | collective-permute-start | bytes 884744 | tf_op jit(solution)/shard_map/ppermute | solution.py:72
  21.9 17.2 %collective-permute-start.9 = (bf16[2,192,384]{2,1,0:T(8,128)(2,1)}, bf16[2,192,384]{2,1,0:T(8,128)(2,1)S(1)}, u32[]{:S(2)}, u32[]{:S(2)}) collective-permute-start(bf16[2,192,384]{2,1,0:T(8,128)(2,1)} %get-tuple-element.53), channel_id=1, source_target_pairs={{0,34},{1,32},{2,2},{3,0},{4,38},{5,36},{6,6},{7,4},{8,42},{9,40},... | collective-permute-start | bytes 884744 | tf_op jit(solution)/shard_map/ppermute | solution.py:72
  30.2 9.6 %collective-permute-start.8 = (bf16[2,192,384]{2,1,0:T(8,128)(2,1)}, bf16[2,192,384]{2,1,0:T(8,128)(2,1)S(1)}, u32[]{:S(2)}, u32[]{:S(2)}) collective-permute-start(bf16[2,192,384]{2,1,0:T(8,128)(2,1)} %get-tuple-element.52), channel_id=1, source_target_pairs={{0,32},{1,34},{2,0},{3,2},{4,36},{5,38},{6,4},{7,6},{8,40},{9,42},... | collective-permute-start | bytes 884744 | tf_op jit(solution)/shard_map/ppermute | solution.py:72
  30.4 9.8 %collective-permute-start.7 = (bf16[2,192,384]{2,1,0:T(8,128)(2,1)S(1)}, bf16[2,192,384]{2,1,0:T(8,128)(2,1)S(1)}, u32[]{:S(2)}, u32[]{:S(2)}) collective-permute-start(bf16[2,192,384]{2,1,0:T(8,128)(2,1)S(1)} %get-tuple-element.51), channel_id=1, source_target_pairs={{0,2},{1,0},{2,34},{3,32},{4,6},{5,4},{6,38},{7,36},{8,10},{9,8},{... | collective-permute-start | bytes 884744 | tf_op jit(solution)/shard_map/ppermute | solution.py:72
  41.4 0.8 copy-start.1
  42.2 18.2 %collective-permute-start.11 = (bf16[2,768,384]{2,1,0:T(8,128)(2,1)}, bf16[2,768,384]{2,1,0:T(8,128)(2,1)}, u32[]{:S(2)}, u32[]{:S(2)}) collective-permute-start(bf16[2,768,384]{2,1,0:T(8,128)(2,1)} %get-tuple-element.54.refs_3_), channel_id=1, source_target_pairs={{1,64},{3,66},{5,68},{7,70},{9,72},{11,74},{13,76},{15,78},{17,80}... | collective-permute-start | bytes 3538952 | tf_op jit(solution)/shard_map/ppermute | solution.py:72
  46.3 14.2 %collective-permute-start.10 = (bf16[2,768,384]{2,1,0:T(8,128)(2,1)}, bf16[2,768,384]{2,1,0:T(8,128)(2,1)}, u32[]{:S(2)}, u32[]{:S(2)}) collective-permute-start(bf16[2,768,384]{2,1,0:T(8,128)(2,1)} %get-tuple-element.54.refs_3_), channel_id=1, source_target_pairs={{0,1},{1,0},{2,3},{3,2},{4,5},{5,4},{6,7},{7,6},{8,9},{9,8},{10,11... | collective-permute-start | bytes 3538952 | tf_op jit(solution)/shard_map/ppermute | solution.py:72
  46.5 32.6 %collective-permute-start.12 = (bf16[2,384,384]{2,1,0:T(8,128)(2,1)}, bf16[2,384,384]{2,1,0:T(8,128)(2,1)S(1)}, u32[]{:S(2)}, u32[]{:S(2)}) collective-permute-start(bf16[2,384,384]{2,1,0:T(8,128)(2,1)} %copy-done.1), channel_id=1, source_target_pairs={{0,16},{1,17},{2,18},{3,19},{4,20},{5,21},{6,22},{7,23},{8,24},{9,... | collective-permute-start | bytes 1769480 | tf_op jit(solution)/shard_map/ppermute | solution.py:72
  79.1 11.2 %collective-permute-start.14 = (bf16[2,384,384]{2,1,0:T(8,128)(2,1)S(1)}, bf16[2,384,384]{2,1,0:T(8,128)(2,1)S(1)}, u32[]{:S(2)}, u32[]{:S(2)}) collective-permute-start(bf16[2,384,384]{2,1,0:T(8,128)(2,1)S(1)} %collective-permute-done.12.refs_1_.refs_2_), channel_id=1, source_target_pairs={{1,64},{3,66},{5,68},{7,70},{9,72},{11,74},{13,76},{15,78},{17,80}... | collective-permute-start | bytes 1769480 | tf_op jit(solution)/shard_map/ppermute | solution.py:72
  81.0 9.3 %collective-permute-start.13 = (bf16[2,384,384]{2,1,0:T(8,128)(2,1)S(1)}, bf16[2,384,384]{2,1,0:T(8,128)(2,1)S(1)}, u32[]{:S(2)}, u32[]{:S(2)}) collective-permute-start(bf16[2,384,384]{2,1,0:T(8,128)(2,1)S(1)} %collective-permute-done.12.refs_1_.refs_2_), channel_id=1, source_target_pairs={{0,1},{1,0},{2,3},{3,2},{4,5},{5,4},{6,7},{7,6},{8,9},{9,8},{10,11... | collective-permute-start | bytes 1769480 | tf_op jit(solution)/shard_map/ppermute | solution.py:72
  94.0 18.3 %collective-permute-start.15 = (bf16[400,768]{1,0:T(8,128)(2,1)S(1)}, bf16[400,768]{1,0:T(8,128)(2,1)S(1)}, u32[]{:S(2)}, u32[]{:S(2)}) collective-permute-start(bf16[400,768]{1,0:T(8,128)(2,1)S(1)} %get-tuple-element.63), channel_id=1, source_target_pairs={{0,4},{1,5},{2,6},{3,7},{4,8},{5,9},{6,10},{7,11},{8,12},{9,13},{1... | collective-permute-start | bytes 1843208 | tf_op jit(solution)/shard_map/ppermute | solution.py:72
  99.0 17.5 %collective-permute-start.16 = (bf16[400,768]{1,0:T(8,128)(2,1)S(1)}, bf16[400,768]{1,0:T(8,128)(2,1)S(1)}, u32[]{:S(2)}, u32[]{:S(2)}) collective-permute-start(bf16[400,768]{1,0:T(8,128)(2,1)S(1)} %get-tuple-element.64), channel_id=1, source_target_pairs={{4,0},{5,1},{6,2},{7,3},{8,4},{9,5},{10,6},{11,7},{12,8},{13,9},{1... | collective-permute-start | bytes 1843208 | tf_op jit(solution)/shard_map/ppermute | solution.py:72
  117.6 9.9 %collective-permute-start.17 = (bf16[192,384]{1,0:T(8,128)(2,1)S(1)}, bf16[192,384]{1,0:T(8,128)(2,1)S(1)}, u32[]{:S(2)}, u32[]{:S(2)}) collective-permute-start(bf16[192,384]{1,0:T(8,128)(2,1)S(1)} %get-tuple-element.65), channel_id=1, source_target_pairs={{0,0},{2,1},{32,2},{34,3},{4,4},{6,5},{36,6},{38,7},{8,8},{10,9},{... | collective-permute-start | bytes 442376 | tf_op jit(solution)/shard_map/ppermute | solution.py:72
  118.2 9.7 %collective-permute-start.18 = (bf16[192,384]{1,0:T(8,128)(2,1)S(1)}, bf16[192,384]{1,0:T(8,128)(2,1)S(1)}, u32[]{:S(2)}, u32[]{:S(2)}) collective-permute-start(bf16[192,384]{1,0:T(8,128)(2,1)S(1)} %get-tuple-element.66), channel_id=1, source_target_pairs={{2,0},{0,1},{34,2},{32,3},{6,4},{4,5},{38,6},{36,7},{10,8},{8,9},{... | collective-permute-start | bytes 442376 | tf_op jit(solution)/shard_map/ppermute | solution.py:72
  122.2 7.1 %collective-permute-start.19 = (bf16[192,384]{1,0:T(8,128)(2,1)S(1)}, bf16[192,384]{1,0:T(8,128)(2,1)S(1)}, u32[]{:S(2)}, u32[]{:S(2)}) collective-permute-start(bf16[192,384]{1,0:T(8,128)(2,1)S(1)} %get-tuple-element.67), channel_id=1, source_target_pairs={{32,0},{34,1},{0,2},{2,3},{36,4},{38,5},{4,6},{6,7},{40,8},{42,9},... | collective-permute-start | bytes 442376 | tf_op jit(solution)/shard_map/ppermute | solution.py:72
  122.9 10.9 %collective-permute-start.20 = (bf16[192,384]{1,0:T(8,128)(2,1)S(1)}, bf16[192,384]{1,0:T(8,128)(2,1)S(1)}, u32[]{:S(2)}, u32[]{:S(2)}) collective-permute-start(bf16[192,384]{1,0:T(8,128)(2,1)S(1)} %get-tuple-element.68), channel_id=1, source_target_pairs={{34,0},{32,1},{2,2},{0,3},{38,4},{36,5},{6,6},{4,7},{42,8},{40,9},... | collective-permute-start | bytes 442376 | tf_op jit(solution)/shard_map/ppermute | solution.py:72
where the time goes:
time: 136 us; the launch traced here: 135 us
  starting transfers between devices  57.9 us (43%)
  waiting for transfers between devices  48.2 us (35%)
  Pallas kernels  23.4 us (17%)
  local copies, waits for them, and re-layouts  2.94 us (2%)
  other arithmetic  2.05 us (2%)
    ppermute x21, starting transfers between devices, send(): return lax.ppermute(x, AXES, pairs)  57.9 us
    ppermute x21, waiting for transfers between devices, send(): return lax.ppermute(x, AXES, pairs)  48.2 us
    pallas_call x3, Pallas kernels, attend(): pl.pallas_call(functools.partial(attend_kernel, sets=sets, pieces=len(sou...  18.4 us
  transfers between devices with their start and end apart: 21, of which 14 were waited for; matrix products, arithmetic and copies ran while one was open for 1% of the time, Pallas kernels for 11%

commit v1 on v0

--- a/solution.py
+++ b/solution.py
@@ -77,33 +77,37 @@
     rows = qkv_ref.shape[1]
     for k in range(4):
         lanes = pl.ds(pl.multiple_of((at_ref[0] ^ k) * width, 128), width)
-        outs[k][:rows, :] = qkv_ref[0, :, lanes]
-        outs[k][rows:, :] = names_ref[...]
-        outs[4 + k][...] = qkv_ref[1:3, :, lanes]
+        for i in range(3):
+            outs[k][i * rows : (i + 1) * rows, :] = qkv_ref[i, :, lanes]
+        outs[k][3 * rows :, :] = names_ref[...]
 
 
 def split(at, qkv, names):
     _, rows, columns = qkv.shape
-    width = columns // 4
     vmem = pl.BlockSpec(memory_space=pltpu.VMEM)
-    shapes = [jax.ShapeDtypeStruct((rows + EXTRA, width), qkv.dtype)] * 4
-    shapes += [jax.ShapeDtypeStruct((2, rows, width), qkv.dtype)] * 4
     return pl.pallas_call(
         split_kernel,
-        out_shape=shapes,
+        out_shape=[jax.ShapeDtypeStruct((3 * rows + EXTRA, columns // 4), qkv.dtype)] * 4,
         in_specs=[pl.BlockSpec(memory_space=pltpu.SMEM), vmem, vmem],
-        out_specs=[vmem] * 8,
+        out_specs=[vmem] * 4,
         compiler_params=pltpu.CompilerParams(vmem_limit_bytes=VMEM_SMALL),
         name="split",
     )(at, qkv, names)
 
 
 def stack_kernel(place_ref, *refs):
-    parts, kv_ref, edge_ref, sems = refs[:4], refs[4], refs[5], refs[6]
-    rows = parts[0].shape[1]
+    parts, (q_ref, kv_ref, edge_ref), sems = refs[:4], refs[4:7], refs[7]
+    rows = (parts[0].shape[0] - EXTRA) // 3
     copies = []
     for k in range(4):
-        copies.append(pltpu.make_async_copy(parts[k], kv_ref.at[:, pl.ds(k * rows, rows)], sems.at[k]))
+        at = pl.ds(k * rows, rows)
+        targets = (q_ref.at[at], kv_ref.at[0, at], kv_ref.at[1, at])
+        for i in range(3):
+            copies.append(
+                pltpu.make_async_copy(parts[k].at[pl.ds(i * rows, rows)], targets[i], sems.at[3 * k + i])
+            )
+    into = q_ref.at[pl.ds(4 * rows, EXTRA)]
+    copies.append(pltpu.make_async_copy(parts[0].at[pl.ds(3 * rows, EXTRA)], into, sems.at[12]))
     for copy in copies:
         copy.start()
     for copy in copies:
@@ -112,48 +116,21 @@
 
 
 def stack(place, parts):
-    _, rows, width = parts[0].shape
+    rows, width = (parts[0].shape[0] - EXTRA) // 3, parts[0].shape[1]
     vmem = pl.BlockSpec(memory_space=pltpu.VMEM)
     return pl.pallas_call(
         stack_kernel,
         out_shape=[
+            jax.ShapeDtypeStruct((4 * rows + EXTRA, width), parts[0].dtype),
             jax.ShapeDtypeStruct((2, 4 * rows, width), parts[0].dtype),
             jax.ShapeDtypeStruct((2, 2 * rows, width), parts[0].dtype),
         ],
         in_specs=[pl.BlockSpec(memory_space=pltpu.SMEM)] + [pl.BlockSpec(memory_space=pl.ANY)] * 4,
-        out_specs=[vmem] * 2,
-        scratch_shapes=[pltpu.SemaphoreType.DMA((4,))],
+        out_specs=[vmem] * 3,
+        scratch_shapes=[pltpu.SemaphoreType.DMA((13,))],
         compiler_params=pltpu.CompilerParams(vmem_limit_bytes=VMEM_SMALL),
         name="stack",
     )(place, *parts)
-
-
-def stack_queries_kernel(*refs):
-    parts, q_ref, sems = refs[:4], refs[4], refs[5]
-    rows = parts[0].shape[0] - EXTRA
-    copies = []
-    for k in range(4):
-        into = q_ref.at[pl.ds(k * rows, rows)]
-        copies.append(pltpu.make_async_copy(parts[k].at[pl.ds(0, rows)], into, sems.at[k]))
-    into = q_ref.at[pl.ds(4 * rows, EXTRA)]
-    copies.append(pltpu.make_async_copy(parts[0].at[pl.ds(rows, EXTRA)], into, sems.at[4]))
-    for copy in copies:
-        copy.start()
-    for copy in copies:
-        copy.wait()
-
-
-def stack_queries(parts):
-    rows, width = parts[0].shape[0] - EXTRA, parts[0].shape[1]
-    return pl.pallas_call(
-        stack_queries_kernel,
-        out_shape=jax.ShapeDtypeStruct((4 * rows + EXTRA, width), parts[0].dtype),
-        in_specs=[pl.BlockSpec(memory_space=pl.ANY)] * 4,
-        out_specs=pl.BlockSpec(memory_space=pltpu.VMEM),
-        scratch_shapes=[pltpu.SemaphoreType.DMA((5,))],
-        compiler_params=pltpu.CompilerParams(vmem_limit_bytes=VMEM_SMALL),
-        name="stack_queries",
-    )(*parts)
 
 
 def join_kernel(at_ref, *refs):
@@ -405,21 +382,15 @@
     names = key_tiles.astype(jnp.bfloat16).reshape(1, entries)
     names = jnp.pad(names, ((0, EXTRA - 1), (0, qkv.shape[2] // 4 - entries)))
     pieces = split(at, qkv, names)
-    q_parts = [send(pieces[k], spread_pairs(k)) for k in range(4)]
-    kv_pieces = list(pieces[4:])
-    for k in range(1, 4):
-        q_parts[k], kv_pieces[k] = lax.optimization_barrier((q_parts[k], kv_pieces[k]))
-    kv_parts = [send(kv_pieces[k], spread_pairs(k)) for k in range(4)]
-    q_own = stack_queries(q_parts)
+    parts = [send(pieces[k], spread_pairs(k)) for k in range(4)]
+    q_own, kv_own, edge = stack(place, parts)
     q_prev = send(q_own, time_pairs(1))
     q_next = send(q_own, time_pairs(-1))
-    place, q_prev, q_next = lax.optimization_barrier((place, q_prev, q_next))
     lists = jnp.stack([q[-EXTRA, :entries] for q in (q_own, q_prev, q_next)])
     lists = lists.astype(jnp.int32).reshape((3,) + key_tiles.shape)
     mask = named(lists, 2 * y + core, pair, time, xh)
     here = jnp.concatenate([jnp.ones((1,), bool), valid])
     mask = (mask & here[:, None, None, None]).astype(jnp.int32).reshape(-1)
-    kv_own, edge = stack(place, kv_parts)
     edge_own = send(edge, edge_pairs())
     bodies = (kv_own, send(kv_own, core_pairs()), send(kv_own, column_pairs()))
 

time: 136 us -> 144 us (1.059); the launches traced: 135 us -> 145 us
  waiting for transfers between devices: 48.2 us -> 71 us
  starting transfers between devices: 57.9 us -> 44 us
  Pallas kernels: 23.4 us -> 25.6 us
    ppermute x21 -> x17, waiting for transfers between devices: 48.2 us -> 71 us  [send(): return lax.ppermute(x, AXES, pairs)]
    ppermute x21 -> x17, starting transfers between devices: 57.9 us -> 44 us  [send(): return lax.ppermute(x, AXES, pairs)]
    pallas_call x3 -> x2, Pallas kernels: 3.03 us -> 4.35 us  [the longest x1 3.43 us: stack(): pl.pallas_call(stack_kernel, out_shape=[jax.ShapeDtypeStruct((4 * rows +...]
  transfers between devices with their start and end apart: 21 -> 17, of which waited for: 14 -> 10; matrix products, arithmetic and copies ran while one was open for 1% -> 1% of each run, Pallas kernels for 11% -> 11%
where the time goes in v1:
time: 144 us; the launch traced here: 145 us
  waiting for transfers between devices  71 us (49%)
  starting transfers between devices  44 us (31%)
  Pallas kernels  25.6 us (18%)
  local copies, waits for them, and re-layouts  2.15 us (1%)
  other arithmetic  2.04 us (1%)
    ppermute x17, waiting for transfers between devices, send(): return lax.ppermute(x, AXES, pairs)  71 us
    ppermute x17, starting transfers between devices, send(): return lax.ppermute(x, AXES, pairs)  44 us
    pallas_call x3, Pallas kernels, attend(): pl.pallas_call(functools.partial(attend_kernel, sets=sets, pieces=len(sou...  19.3 us
    pallas_call x1, Pallas kernels, stack(): pl.pallas_call(stack_kernel, out_shape=[jax.ShapeDtypeStruct((4 * rows +...  3.43 us
  transfers between devices with their start and end apart: 17, of which 10 were waited for; matrix products, arithmetic and copies ran while one was open for 1% of the time, Pallas kernels for 11%

profile of v1, /device:TPU:8, one launch (start us, length us, event | category | flops | bytes accessed | tf_op | source)
XLA Modules:
  0.0 145.2 jit_solution(10271570224955054367)
XLA Ops:
  0.0 0.7 convert_element_type.18
  0.7 0.1 reshape.128
  0.8 0.0 copy-start
  0.8 1.5 %copy-done = bf16[3,192,1536]{2,1,0:T(8,128)(2,1)S(1)} copy-done((bf16[3,192,1536]{2,1,0:T(8,128)(2,1)S(1)}, bf16[3,192,1536]{2,1,0:T(8,128)(2,1)}, u32[]{:S(2)}) %copy-start) | copy-done | bytes 1769496
  2.3 0.9 split.1
  3.2 1.7 %collective-permute-start = (bf16[592,384]{1,0:T(8,128)(2,1)}, bf16[592,384]{1,0:T(8,128)(2,1)S(1)}, u32[]{:S(2)}, u32[]{:S(2)}) collective-permute-start(bf16[592,384]{1,0:T(8,128)(2,1)} %get-tuple-element.25), channel_id=1, source_target_pairs={{0,0},{1,2},{2,32},{3,34},{4,4},{5,6},{6,36},{7,38},{8,8},{9,10},{... | collective-permute-start | bytes 1363976 | tf_op jit(solution)/shard_map/ppermute | solution.py:72
  4.9 3.3 %collective-permute-start.1 = (bf16[592,384]{1,0:T(8,128)(2,1)S(1)}, bf16[592,384]{1,0:T(8,128)(2,1)S(1)}, u32[]{:S(2)}, u32[]{:S(2)}) collective-permute-start(bf16[592,384]{1,0:T(8,128)(2,1)S(1)} %get-tuple-element.26), channel_id=1, source_target_pairs={{0,2},{1,0},{2,34},{3,32},{4,6},{5,4},{6,38},{7,36},{8,10},{9,8},{... | collective-permute-start | bytes 1363976 | tf_op jit(solution)/shard_map/ppermute | solution.py:72
  8.2 2.4 %collective-permute-start.2 = (bf16[592,384]{1,0:T(8,128)(2,1)S(1)}, bf16[592,384]{1,0:T(8,128)(2,1)S(1)}, u32[]{:S(2)}, u32[]{:S(2)}) collective-permute-start(bf16[592,384]{1,0:T(8,128)(2,1)S(1)} %get-tuple-element.27), channel_id=1, source_target_pairs={{0,32},{1,34},{2,0},{3,2},{4,36},{5,38},{6,4},{7,6},{8,40},{9,42},... | collective-permute-start | bytes 1363976 | tf_op jit(solution)/shard_map/ppermute | solution.py:72
  10.6 1.9 %collective-permute-start.3 = (bf16[592,384]{1,0:T(8,128)(2,1)S(1)}, bf16[592,384]{1,0:T(8,128)(2,1)S(1)}, u32[]{:S(2)}, u32[]{:S(2)}) collective-permute-start(bf16[592,384]{1,0:T(8,128)(2,1)S(1)} %get-tuple-element.28), channel_id=1, source_target_pairs={{0,34},{1,32},{2,2},{3,0},{4,38},{5,36},{6,6},{7,4},{8,42},{9,40},... | collective-permute-start | bytes 1363976 | tf_op jit(solution)/shard_map/ppermute | solution.py:72
  12.6 6.5 %collective-permute-done.1.refs_1_ = bf16[592,384]{1,0:T(8,128)(2,1)S(1)} collective-permute-done((bf16[592,384]{1,0:T(8,128)(2,1)S(1)}, bf16[592,384]{1,0:T(8,128)(2,1)S(1)}, u32[]{:S(2)}, u32[]{:S(2)}) %collective-permute-start.1) | collective-permute-done | bytes 454688 | tf_op jit(solution)/shard_map/ppermute | solution.py:72
  19.0 10.3 %collective-permute-done.2.refs_2_ = bf16[592,384]{1,0:T(8,128)(2,1)S(1)} collective-permute-done((bf16[592,384]{1,0:T(8,128)(2,1)S(1)}, bf16[592,384]{1,0:T(8,128)(2,1)S(1)}, u32[]{:S(2)}, u32[]{:S(2)}) %collective-permute-start.2) | collective-permute-done | bytes 454688 | tf_op jit(solution)/shard_map/ppermute | solution.py:72
  29.4 0.0 collective-permute-done.3.refs_3_
  29.4 3.4 %stack.26 = (bf16[784,384]{1,0:T(8,128)(2,1)S(1)}, bf16[2,768,384]{2,1,0:T(8,128)(2,1)}, bf16[2,384,384]{2,1,0:T(8,128)(2,1)S(1)}) custom-call(s32[1]{0:T(128)} %bitcast.3.place_ref, bf16[592,384]{1,0:T(8,128)(2,1)S(1)} %collective-permute-done.refs_0_, bf16[592,384]{1,0:T(8,128)(2,1)S(1)} %collective-permute-done.1.refs_1_, ...), custom_call_target="tpu_custom_call" | custom-call | tf_op jit(solution)/shard_map/stack/pallas_call | solution.py:121
  32.8 1.3 collective-permute-start.5
  34.1 1.9 %collective-permute-start.7 = (bf16[2,768,384]{2,1,0:T(8,128)(2,1)}, bf16[2,768,384]{2,1,0:T(8,128)(2,1)}, u32[]{:S(2)}, u32[]{:S(2)}) collective-permute-start(bf16[2,768,384]{2,1,0:T(8,128)(2,1)} %get-tuple-element.30.refs_3_), channel_id=1, source_target_pairs={{1,64},{3,66},{5,68},{7,70},{9,72},{11,74},{13,76},{15,78},{17,80}... | collective-permute-start | bytes 3538952 | tf_op jit(solution)/shard_map/ppermute | solution.py:72
  36.1 1.8 %collective-permute-start.6 = (bf16[2,768,384]{2,1,0:T(8,128)(2,1)}, bf16[2,768,384]{2,1,0:T(8,128)(2,1)}, u32[]{:S(2)}, u32[]{:S(2)}) collective-permute-start(bf16[2,768,384]{2,1,0:T(8,128)(2,1)} %get-tuple-element.30.refs_3_), channel_id=1, source_target_pairs={{0,1},{1,0},{2,3},{3,2},{4,5},{5,4},{6,7},{7,6},{8,9},{9,8},{10,11... | collective-permute-start | bytes 3538952 | tf_op jit(solution)/shard_map/ppermute | solution.py:72
  37.8 4.6 %collective-permute-start.4 = (bf16[784,384]{1,0:T(8,128)(2,1)S(1)}, bf16[784,384]{1,0:T(8,128)(2,1)S(1)}, u32[]{:S(2)}, u32[]{:S(2)}) collective-permute-start(bf16[784,384]{1,0:T(8,128)(2,1)S(1)} %get-tuple-element.29.refs_0_), channel_id=1, source_target_pairs={{0,4},{1,5},{2,6},{3,7},{4,8},{5,9},{6,10},{7,11},{8,12},{9,13},{1... | collective-permute-start | bytes 1806344 | tf_op jit(solution)/shard_map/ppermute | solution.py:72
  42.5 0.1 pad_add_fusion
  42.6 0.1 stack.22
  42.7 7.2 %collective-permute-start.8 = (bf16[2,384,384]{2,1,0:T(8,128)(2,1)S(1)}, bf16[2,384,384]{2,1,0:T(8,128)(2,1)S(1)}, u32[]{:S(2)}, u32[]{:S(2)}) collective-permute-start(bf16[2,384,384]{2,1,0:T(8,128)(2,1)S(1)} %get-tuple-element.34), channel_id=1, source_target_pairs={{0,16},{1,17},{2,18},{3,19},{4,20},{5,21},{6,22},{7,23},{8,24},{9,... | collective-permute-start | bytes 1769480 | tf_op jit(solution)/shard_map/ppermute | solution.py:72
  49.9 0.3 collective-permute-done.5.refs_2_.refs_1_
  50.2 0.1 stack.24
  50.3 6.1 %collective-permute-done.4.refs_1_.refs_0_ = bf16[784,384]{1,0:T(8,128)(2,1)S(1)} collective-permute-done((bf16[784,384]{1,0:T(8,128)(2,1)S(1)}, bf16[784,384]{1,0:T(8,128)(2,1)S(1)}, u32[]{:S(2)}, u32[]{:S(2)}) %collective-permute-start.4) | collective-permute-done | bytes 602144 | tf_op jit(solution)/shard_map/ppermute | solution.py:72
  56.4 0.1 stack.23
  56.4 0.1 fusion.2
  56.6 1.0 fusion
  57.6 0.1 copy.7
  57.7 0.1 fusion.4
  57.8 0.1 reshape.132.mask_ref
  57.9 12.8 %attend_3_6.1 = (f32[400,768]{1,0:T(8,128)S(1)}, f32[400,768]{1,0:T(8,128)S(1)}, f32[400,768]{1,0:T(8,128)S(1)}) custom-call(s32[162]{0:T(256)S(1)} %reshape.132.mask_ref, bf16[784,384]{1,0:T(8,128)(2,1)S(1)} %get-tuple-element.29.refs_0_, bf16[784,384]{1,0:T(8,128)(2,1)S(1)} %collective-permute-done.4.refs_1_.refs_0_, ...), custom_call_target="tpu_custom_call" | custom-call | tf_op jit(solution)/shard_map/attend_3_6/pallas_call | solution.py:286
  70.7 17.6 %collective-permute-done.8.refs_1_.refs_2_ = bf16[2,384,384]{2,1,0:T(8,128)(2,1)S(1)} collective-permute-done((bf16[2,384,384]{2,1,0:T(8,128)(2,1)S(1)}, bf16[2,384,384]{2,1,0:T(8,128)(2,1)S(1)}, u32[]{:S(2)}, u32[]{:S(2)}) %collective-permute-start.8) | collective-permute-done | bytes 589856 | tf_op jit(solution)/shard_map/ppermute | solution.py:72
  88.3 1.9 %collective-permute-start.10 = (bf16[2,384,384]{2,1,0:T(8,128)(2,1)S(1)}, bf16[2,384,384]{2,1,0:T(8,128)(2,1)S(1)}, u32[]{:S(2)}, u32[]{:S(2)}) collective-permute-start(bf16[2,384,384]{2,1,0:T(8,128)(2,1)S(1)} %collective-permute-done.8.refs_1_.refs_2_), channel_id=1, source_target_pairs={{1,64},{3,66},{5,68},{7,70},{9,72},{11,74},{13,76},{15,78},{17,80}... | collective-permute-start | bytes 1769480 | tf_op jit(solution)/shard_map/ppermute | solution.py:72
  90.2 1.5 %collective-permute-start.9 = (bf16[2,384,384]{2,1,0:T(8,128)(2,1)S(1)}, bf16[2,384,384]{2,1,0:T(8,128)(2,1)S(1)}, u32[]{:S(2)}, u32[]{:S(2)}) collective-permute-start(bf16[2,384,384]{2,1,0:T(8,128)(2,1)S(1)} %collective-permute-done.8.refs_1_.refs_2_), channel_id=1, source_target_pairs={{0,1},{1,0},{2,3},{3,2},{4,5},{5,4},{6,7},{7,6},{8,9},{9,8},{10,11... | collective-permute-start | bytes 1769480 | tf_op jit(solution)/shard_map/ppermute | solution.py:72
  91.7 7.8 %collective-permute-done.10.refs_3_.refs_4_ = bf16[2,384,384]{2,1,0:T(8,128)(2,1)S(1)} collective-permute-done((bf16[2,384,384]{2,1,0:T(8,128)(2,1)S(1)}, bf16[2,384,384]{2,1,0:T(8,128)(2,1)S(1)}, u32[]{:S(2)}, u32[]{:S(2)}) %collective-permute-start.10) | collective-permute-done | bytes 589856 | tf_op jit(solution)/shard_map/ppermute | solution.py:72
  99.5 3.5 %attend_2_3.1 = (bf16[400,768]{1,0:T(8,128)(2,1)S(1)}, bf16[400,768]{1,0:T(8,128)(2,1)S(1)}) custom-call(s32[162]{0:T(256)S(1)} %reshape.132.mask_ref, bf16[784,384]{1,0:T(8,128)(2,1)S(1)} %collective-permute-done.4.refs_1_.refs_0_, bf16[784,384]{1,0:T(8,128)(2,1)S(1)} %collective-permute-done.5.refs_2_.refs_1_, ...), custom_call_target="tpu_custom_call" | custom-call | tf_op jit(solution)/shard_map/attend_2_3/pallas_call | solution.py:286
  103.1 5.1 %collective-permute-start.11 = (bf16[400,768]{1,0:T(8,128)(2,1)S(1)}, bf16[400,768]{1,0:T(8,128)(2,1)S(1)}, u32[]{:S(2)}, u32[]{:S(2)}) collective-permute-start(bf16[400,768]{1,0:T(8,128)(2,1)S(1)} %get-tuple-element.39), channel_id=1, source_target_pairs={{0,4},{1,5},{2,6},{3,7},{4,8},{5,9},{6,10},{7,11},{8,12},{9,13},{1... | collective-permute-start | bytes 1843208 | tf_op jit(solution)/shard_map/ppermute | solution.py:72
  108.2 1.3 collective-permute-start.12
  109.5 0.1 add_convert_fusion.valid_ref
  109.5 3.0 %attend_1_3.1.refs_0_ = f32[400,768]{1,0:T(8,128)S(1)} custom-call(s32[162]{0:T(256)S(1)} %reshape.132.mask_ref, bf16[784,384]{1,0:T(8,128)(2,1)S(1)} %get-tuple-element.29.refs_0_, bf16[2,384,384]{2,1,0:T(8,128)(2,1)S(1)} %collective-permute-done.8.refs_1_.refs_2_, bf16[2,384,384]{2,1,0:T(8,128)(2,1)S(1)} %collective-permute-done.9.refs_2_.refs_3_, ...), custom_call_target="tpu_custom_call" | custom-call | tf_op jit(solution)/shard_map/attend_1_3/pallas_call | solution.py:286
  112.6 8.8 %collective-permute-done.11.refs_1_ = bf16[400,768]{1,0:T(8,128)(2,1)S(1)} collective-permute-done((bf16[400,768]{1,0:T(8,128)(2,1)S(1)}, bf16[400,768]{1,0:T(8,128)(2,1)S(1)}, u32[]{:S(2)}, u32[]{:S(2)}) %collective-permute-start.11) | collective-permute-done | bytes 614432 | tf_op jit(solution)/shard_map/ppermute | solution.py:72
  121.3 4.8 %collective-permute-done.12.refs_2_ = bf16[400,768]{1,0:T(8,128)(2,1)S(1)} collective-permute-done((bf16[400,768]{1,0:T(8,128)(2,1)S(1)}, bf16[400,768]{1,0:T(8,128)(2,1)S(1)}, u32[]{:S(2)}, u32[]{:S(2)}) %collective-permute-start.12) | collective-permute-done | bytes 614432 | tf_op jit(solution)/shard_map/ppermute | solution.py:72
  126.2 1.1 merge.1
  127.2 0.7 collective-permute-start.13
  127.9 4.4 %collective-permute-start.14 = (bf16[192,384]{1,0:T(8,128)(2,1)S(1)}, bf16[192,384]{1,0:T(8,128)(2,1)S(1)}, u32[]{:S(2)}, u32[]{:S(2)}) collective-permute-start(bf16[192,384]{1,0:T(8,128)(2,1)S(1)} %get-tuple-element.42), channel_id=1, source_target_pairs={{2,0},{0,1},{34,2},{32,3},{6,4},{4,5},{38,6},{36,7},{10,8},{8,9},{... | collective-permute-start | bytes 442376 | tf_op jit(solution)/shard_map/ppermute | solution.py:72
  132.3 3.1 %collective-permute-start.16 = (bf16[192,384]{1,0:T(8,128)(2,1)S(1)}, bf16[192,384]{1,0:T(8,128)(2,1)S(1)}, u32[]{:S(2)}, u32[]{:S(2)}) collective-permute-start(bf16[192,384]{1,0:T(8,128)(2,1)S(1)} %get-tuple-element.44), channel_id=1, source_target_pairs={{34,0},{32,1},{2,2},{0,3},{38,4},{36,5},{6,6},{4,7},{42,8},{40,9},... | collective-permute-start | bytes 442376 | tf_op jit(solution)/shard_map/ppermute | solution.py:72
  135.5 4.5 %collective-permute-done.15.refs_2_ = bf16[192,384]{1,0:T(8,128)(2,1)S(1)} collective-permute-done((bf16[192,384]{1,0:T(8,128)(2,1)S(1)}, bf16[192,384]{1,0:T(8,128)(2,1)S(1)}, u32[]{:S(2)}, u32[]{:S(2)}) %collective-permute-start.15) | collective-permute-done | bytes 147488 | tf_op jit(solution)/shard_map/ppermute | solution.py:72
  140.0 4.3 %collective-permute-done.16.refs_3_ = bf16[192,384]{1,0:T(8,128)(2,1)S(1)} collective-permute-done((bf16[192,384]{1,0:T(8,128)(2,1)S(1)}, bf16[192,384]{1,0:T(8,128)(2,1)S(1)}, u32[]{:S(2)}, u32[]{:S(2)}) %collective-permute-start.16) | collective-permute-done | bytes 147488 | tf_op jit(solution)/shard_map/ppermute | solution.py:72
  144.3 0.9 join.1
  (13 shorter events, 0.1 us)
Async XLA Ops:
  0.8 1.5 %copy-start = (bf16[3,192,1536]{2,1,0:T(8,128)(2,1)S(1)}, bf16[3,192,1536]{2,1,0:T(8,128)(2,1)}, u32[]{:S(2)}) copy-start(bf16[3,192,1536]{2,1,0:T(8,128)(2,1)} %qkv_ref.1) | copy-start | bytes 5308420
  3.2 9.4 %collective-permute-start = (bf16[592,384]{1,0:T(8,128)(2,1)}, bf16[592,384]{1,0:T(8,128)(2,1)S(1)}, u32[]{:S(2)}, u32[]{:S(2)}) collective-permute-start(bf16[592,384]{1,0:T(8,128)(2,1)} %get-tuple-element.25), channel_id=1, source_target_pairs={{0,0},{1,2},{2,32},{3,34},{4,4},{5,6},{6,36},{7,38},{8,8},{9,10},{... | collective-permute-start | bytes 1363976 | tf_op jit(solution)/shard_map/ppermute | solution.py:72
  4.9 14.2 %collective-permute-start.1 = (bf16[592,384]{1,0:T(8,128)(2,1)S(1)}, bf16[592,384]{1,0:T(8,128)(2,1)S(1)}, u32[]{:S(2)}, u32[]{:S(2)}) collective-permute-start(bf16[592,384]{1,0:T(8,128)(2,1)S(1)} %get-tuple-element.26), channel_id=1, source_target_pairs={{0,2},{1,0},{2,34},{3,32},{4,6},{5,4},{6,38},{7,36},{8,10},{9,8},{... | collective-permute-start | bytes 1363976 | tf_op jit(solution)/shard_map/ppermute | solution.py:72
  8.2 21.2 %collective-permute-start.2 = (bf16[592,384]{1,0:T(8,128)(2,1)S(1)}, bf16[592,384]{1,0:T(8,128)(2,1)S(1)}, u32[]{:S(2)}, u32[]{:S(2)}) collective-permute-start(bf16[592,384]{1,0:T(8,128)(2,1)S(1)} %get-tuple-element.27), channel_id=1, source_target_pairs={{0,32},{1,34},{2,0},{3,2},{4,36},{5,38},{6,4},{7,6},{8,40},{9,42},... | collective-permute-start | bytes 1363976 | tf_op jit(solution)/shard_map/ppermute | solution.py:72
  10.6 18.8 %collective-permute-start.3 = (bf16[592,384]{1,0:T(8,128)(2,1)S(1)}, bf16[592,384]{1,0:T(8,128)(2,1)S(1)}, u32[]{:S(2)}, u32[]{:S(2)}) collective-permute-start(bf16[592,384]{1,0:T(8,128)(2,1)S(1)} %get-tuple-element.28), channel_id=1, source_target_pairs={{0,34},{1,32},{2,2},{3,0},{4,38},{5,36},{6,6},{7,4},{8,42},{9,40},... | collective-permute-start | bytes 1363976 | tf_op jit(solution)/shard_map/ppermute | solution.py:72
  32.8 17.3 %collective-permute-start.5 = (bf16[784,384]{1,0:T(8,128)(2,1)S(1)}, bf16[784,384]{1,0:T(8,128)(2,1)S(1)}, u32[]{:S(2)}, u32[]{:S(2)}) collective-permute-start(bf16[784,384]{1,0:T(8,128)(2,1)S(1)} %get-tuple-element.29.refs_0_), channel_id=1, source_target_pairs={{4,0},{5,1},{6,2},{7,3},{8,4},{9,5},{10,6},{11,7},{12,8},{13,9},{1... | collective-permute-start | bytes 1806344 | tf_op jit(solution)/shard_map/ppermute | solution.py:72
  34.1 23.8 %collective-permute-start.7 = (bf16[2,768,384]{2,1,0:T(8,128)(2,1)}, bf16[2,768,384]{2,1,0:T(8,128)(2,1)}, u32[]{:S(2)}, u32[]{:S(2)}) collective-permute-start(bf16[2,768,384]{2,1,0:T(8,128)(2,1)} %get-tuple-element.30.refs_3_), channel_id=1, source_target_pairs={{1,64},{3,66},{5,68},{7,70},{9,72},{11,74},{13,76},{15,78},{17,80}... | collective-permute-start | bytes 3538952 | tf_op jit(solution)/shard_map/ppermute | solution.py:72
  36.1 21.9 %collective-permute-start.6 = (bf16[2,768,384]{2,1,0:T(8,128)(2,1)}, bf16[2,768,384]{2,1,0:T(8,128)(2,1)}, u32[]{:S(2)}, u32[]{:S(2)}) collective-permute-start(bf16[2,768,384]{2,1,0:T(8,128)(2,1)} %get-tuple-element.30.refs_3_), channel_id=1, source_target_pairs={{0,1},{1,0},{2,3},{3,2},{4,5},{5,4},{6,7},{7,6},{8,9},{9,8},{10,11... | collective-permute-start | bytes 3538952 | tf_op jit(solution)/shard_map/ppermute | solution.py:72
  37.8 18.5 %collective-permute-start.4 = (bf16[784,384]{1,0:T(8,128)(2,1)S(1)}, bf16[784,384]{1,0:T(8,128)(2,1)S(1)}, u32[]{:S(2)}, u32[]{:S(2)}) collective-permute-start(bf16[784,384]{1,0:T(8,128)(2,1)S(1)} %get-tuple-element.29.refs_0_), channel_id=1, source_target_pairs={{0,4},{1,5},{2,6},{3,7},{4,8},{5,9},{6,10},{7,11},{8,12},{9,13},{1... | collective-permute-start | bytes 1806344 | tf_op jit(solution)/shard_map/ppermute | solution.py:72
  42.7 45.7 %collective-permute-start.8 = (bf16[2,384,384]{2,1,0:T(8,128)(2,1)S(1)}, bf16[2,384,384]{2,1,0:T(8,128)(2,1)S(1)}, u32[]{:S(2)}, u32[]{:S(2)}) collective-permute-start(bf16[2,384,384]{2,1,0:T(8,128)(2,1)S(1)} %get-tuple-element.34), channel_id=1, source_target_pairs={{0,16},{1,17},{2,18},{3,19},{4,20},{5,21},{6,22},{7,23},{8,24},{9,... | collective-permute-start | bytes 1769480 | tf_op jit(solution)/shard_map/ppermute | solution.py:72
  88.3 11.2 %collective-permute-start.10 = (bf16[2,384,384]{2,1,0:T(8,128)(2,1)S(1)}, bf16[2,384,384]{2,1,0:T(8,128)(2,1)S(1)}, u32[]{:S(2)}, u32[]{:S(2)}) collective-permute-start(bf16[2,384,384]{2,1,0:T(8,128)(2,1)S(1)} %collective-permute-done.8.refs_1_.refs_2_), channel_id=1, source_target_pairs={{1,64},{3,66},{5,68},{7,70},{9,72},{11,74},{13,76},{15,78},{17,80}... | collective-permute-start | bytes 1769480 | tf_op jit(solution)/shard_map/ppermute | solution.py:72
  90.2 9.3 %collective-permute-start.9 = (bf16[2,384,384]{2,1,0:T(8,128)(2,1)S(1)}, bf16[2,384,384]{2,1,0:T(8,128)(2,1)S(1)}, u32[]{:S(2)}, u32[]{:S(2)}) collective-permute-start(bf16[2,384,384]{2,1,0:T(8,128)(2,1)S(1)} %collective-permute-done.8.refs_1_.refs_2_), channel_id=1, source_target_pairs={{0,1},{1,0},{2,3},{3,2},{4,5},{5,4},{6,7},{7,6},{8,9},{9,8},{10,11... | collective-permute-start | bytes 1769480 | tf_op jit(solution)/shard_map/ppermute | solution.py:72
  103.1 18.3 %collective-permute-start.11 = (bf16[400,768]{1,0:T(8,128)(2,1)S(1)}, bf16[400,768]{1,0:T(8,128)(2,1)S(1)}, u32[]{:S(2)}, u32[]{:S(2)}) collective-permute-start(bf16[400,768]{1,0:T(8,128)(2,1)S(1)} %get-tuple-element.39), channel_id=1, source_target_pairs={{0,4},{1,5},{2,6},{3,7},{4,8},{5,9},{6,10},{7,11},{8,12},{9,13},{1... | collective-permute-start | bytes 1843208 | tf_op jit(solution)/shard_map/ppermute | solution.py:72
  108.2 18.0 %collective-permute-start.12 = (bf16[400,768]{1,0:T(8,128)(2,1)S(1)}, bf16[400,768]{1,0:T(8,128)(2,1)S(1)}, u32[]{:S(2)}, u32[]{:S(2)}) collective-permute-start(bf16[400,768]{1,0:T(8,128)(2,1)S(1)} %get-tuple-element.40), channel_id=1, source_target_pairs={{4,0},{5,1},{6,2},{7,3},{8,4},{9,5},{10,6},{11,7},{12,8},{13,9},{1... | collective-permute-start | bytes 1843208 | tf_op jit(solution)/shard_map/ppermute | solution.py:72
  127.2 8.2 %collective-permute-start.13 = (bf16[192,384]{1,0:T(8,128)(2,1)S(1)}, bf16[192,384]{1,0:T(8,128)(2,1)S(1)}, u32[]{:S(2)}, u32[]{:S(2)}) collective-permute-start(bf16[192,384]{1,0:T(8,128)(2,1)S(1)} %get-tuple-element.41), channel_id=1, source_target_pairs={{0,0},{2,1},{32,2},{34,3},{4,4},{6,5},{36,6},{38,7},{8,8},{10,9},{... | collective-permute-start | bytes 442376 | tf_op jit(solution)/shard_map/ppermute | solution.py:72
  127.9 7.5 %collective-permute-start.14 = (bf16[192,384]{1,0:T(8,128)(2,1)S(1)}, bf16[192,384]{1,0:T(8,128)(2,1)S(1)}, u32[]{:S(2)}, u32[]{:S(2)}) collective-permute-start(bf16[192,384]{1,0:T(8,128)(2,1)S(1)} %get-tuple-element.42), channel_id=1, source_target_pairs={{2,0},{0,1},{34,2},{32,3},{6,4},{4,5},{38,6},{36,7},{10,8},{8,9},{... | collective-permute-start | bytes 442376 | tf_op jit(solution)/shard_map/ppermute | solution.py:72
  132.3 7.7 %collective-permute-start.15 = (bf16[192,384]{1,0:T(8,128)(2,1)S(1)}, bf16[192,384]{1,0:T(8,128)(2,1)S(1)}, u32[]{:S(2)}, u32[]{:S(2)}) collective-permute-start(bf16[192,384]{1,0:T(8,128)(2,1)S(1)} %get-tuple-element.43), channel_id=1, source_target_pairs={{32,0},{34,1},{0,2},{2,3},{36,4},{38,5},{4,6},{6,7},{40,8},{42,9},... | collective-permute-start | bytes 442376 | tf_op jit(solution)/shard_map/ppermute | solution.py:72
  132.3 12.0 %collective-permute-start.16 = (bf16[192,384]{1,0:T(8,128)(2,1)S(1)}, bf16[192,384]{1,0:T(8,128)(2,1)S(1)}, u32[]{:S(2)}, u32[]{:S(2)}) collective-permute-start(bf16[192,384]{1,0:T(8,128)(2,1)S(1)} %get-tuple-element.44), channel_id=1, source_target_pairs={{34,0},{32,1},{2,2},{0,3},{38,4},{36,5},{6,6},{4,7},{42,8},{40,9},... | collective-permute-start | bytes 442376 | tf_op jit(solution)/shard_map/ppermute | solution.py:72

commit v2 on v0

--- a/solution.py
+++ b/solution.py
@@ -423,13 +423,13 @@
     edge_own = send(edge, edge_pairs())
     bodies = (kv_own, send(kv_own, core_pairs()), send(kv_own, column_pairs()))
 
-    begun = attend(mask, (q_own, q_prev, q_next), bodies, (), heads, 0, 0, jnp.float32)
+    begun = attend(mask, (q_prev, q_next), bodies, (), heads, 1, 0, jnp.float32)
     begun, edge_own = lax.optimization_barrier((begun, edge_own))
     edges = (edge_own, send(edge_own, core_pairs()), send(edge_own, column_pairs()))
-    o_prev, o_next = attend(mask, (q_prev, q_next), edges, begun[1:], heads, 1, 6, jnp.bfloat16)
+    o_prev, o_next = attend(mask, (q_prev, q_next), edges, begun, heads, 1, 6, jnp.bfloat16)
     o_before = send(o_next, time_pairs(1))
     o_after = send(o_prev, time_pairs(-1))
-    (o_own,) = attend(mask, (q_own,), edges, begun[:1], heads, 0, 6, jnp.float32)
+    (o_own,) = attend(mask, (q_own,), bodies + edges, (), heads, 0, 0, jnp.float32)
 
     chunks = merge(valid.astype(jnp.int32), (o_own, o_before, o_after), heads)
     home = [send(chunks[k], gather_pairs(k)) for k in range(4)]

time: 136 us -> 137 us (level)
  local copies, waits for them, and re-layouts: 2.94 us -> 5.36 us
  starting transfers between devices: 57.9 us -> 55.7 us
    ppermute x21, starting transfers between devices: 57.9 us -> 55.7 us  [send(): return lax.ppermute(x, AXES, pairs)]
    unnamed x4 -> x14, local copies, waits for them, and re-layouts: 2.28 us -> 3.37 us
  transfers between devices with their start and end apart: 21 -> 21, of which waited for: 14 -> 14; matrix products, arithmetic and copies ran while one was open for 1% -> 3% of each run, Pallas kernels for 11% -> 11%
where the time goes in v2:
time: 137 us; the launch traced here: 135 us
  starting transfers between devices  55.7 us (41%)
  waiting for transfers between devices  47.8 us (35%)
  Pallas kernels  22.7 us (17%)
  local copies, waits for them, and re-layouts  5.36 us (4%)
  other arithmetic  3.15 us (2%)
    ppermute x21, starting transfers between devices, send(): return lax.ppermute(x, AXES, pairs)  55.7 us
    ppermute x21, waiting for transfers between devices, send(): return lax.ppermute(x, AXES, pairs)  47.8 us
    pallas_call x3, Pallas kernels, attend(): pl.pallas_call(functools.partial(attend_kernel, sets=sets, pieces=len(sou...  18.9 us
    unnamed x14, local copies, waits for them, and re-layouts  3.37 us
  transfers between devices with their start and end apart: 21, of which 14 were waited for; matrix products, arithmetic and copies ran while one was open for 3% of the time, Pallas kernels for 11%

profile of v2, /device:TPU:8, one launch (start us, length us, event | category | flops | bytes accessed | tf_op | source)
XLA Modules:
  0.0 135.1 jit_solution(9932386426773089337)
XLA Ops:
  0.0 0.7 convert_element_type.18
  0.8 1.5 %copy-done.5 = bf16[3,192,1536]{2,1,0:T(8,128)(2,1)S(1)} copy-done((bf16[3,192,1536]{2,1,0:T(8,128)(2,1)S(1)}, bf16[3,192,1536]{2,1,0:T(8,128)(2,1)}, u32[]{:S(2)}) %copy-start.5) | copy-done | bytes 1769496
  2.3 0.9 split.1
  3.1 1.5 %collective-permute-start.1 = (bf16[208,384]{1,0:T(8,128)(2,1)S(1)}, bf16[208,384]{1,0:T(8,128)(2,1)S(1)}, u32[]{:S(2)}, u32[]{:S(2)}) collective-permute-start(bf16[208,384]{1,0:T(8,128)(2,1)S(1)} %get-tuple-element.36), channel_id=1, source_target_pairs={{0,2},{1,0},{2,34},{3,32},{4,6},{5,4},{6,38},{7,36},{8,10},{9,8},{... | collective-permute-start | bytes 479240 | tf_op jit(solution)/shard_map/ppermute | solution.py:72
  4.6 1.5 %collective-permute-start.2 = (bf16[208,384]{1,0:T(8,128)(2,1)S(1)}, bf16[208,384]{1,0:T(8,128)(2,1)S(1)}, u32[]{:S(2)}, u32[]{:S(2)}) collective-permute-start(bf16[208,384]{1,0:T(8,128)(2,1)S(1)} %get-tuple-element.39), channel_id=1, source_target_pairs={{0,32},{1,34},{2,0},{3,2},{4,36},{5,38},{6,4},{7,6},{8,40},{9,42},... | collective-permute-start | bytes 479240 | tf_op jit(solution)/shard_map/ppermute | solution.py:72
  6.2 2.2 %collective-permute-start.3 = (bf16[208,384]{1,0:T(8,128)(2,1)S(1)}, bf16[208,384]{1,0:T(8,128)(2,1)S(1)}, u32[]{:S(2)}, u32[]{:S(2)}) collective-permute-start(bf16[208,384]{1,0:T(8,128)(2,1)S(1)} %get-tuple-element.42), channel_id=1, source_target_pairs={{0,34},{1,32},{2,2},{3,0},{4,38},{5,36},{6,6},{7,4},{8,42},{9,40},... | collective-permute-start | bytes 479240 | tf_op jit(solution)/shard_map/ppermute | solution.py:72
  8.4 0.7 collective-permute-start
  9.1 3.3 %collective-permute-done.2.refs_2_ = bf16[208,384]{1,0:T(8,128)(2,1)S(1)} collective-permute-done((bf16[208,384]{1,0:T(8,128)(2,1)S(1)}, bf16[208,384]{1,0:T(8,128)(2,1)S(1)}, u32[]{:S(2)}, u32[]{:S(2)}) %collective-permute-start.2) | collective-permute-done | bytes 159776 | tf_op jit(solution)/shard_map/ppermute | solution.py:72
  12.4 1.1 collective-permute-done.3.refs_3_
  13.5 0.8 stack_queries.1.refs_0_
  14.3 1.3 collective-permute-start.5
  15.6 4.6 %collective-permute-start.4 = (bf16[784,384]{1,0:T(8,128)(2,1)S(1)}, bf16[784,384]{1,0:T(8,128)(2,1)S(1)}, u32[]{:S(2)}, u32[]{:S(2)}) collective-permute-start(bf16[784,384]{1,0:T(8,128)(2,1)S(1)} %stack_queries.1.refs_0_), channel_id=1, source_target_pairs={{0,4},{1,5},{2,6},{3,7},{4,8},{5,9},{6,10},{7,11},{8,12},{9,13},{1... | collective-permute-start | bytes 1806344 | tf_op jit(solution)/shard_map/ppermute | solution.py:72
  20.2 1.6 %collective-permute-start.6 = (bf16[2,192,384]{2,1,0:T(8,128)(2,1)}, bf16[2,192,384]{2,1,0:T(8,128)(2,1)S(1)}, u32[]{:S(2)}, u32[]{:S(2)}) collective-permute-start(bf16[2,192,384]{2,1,0:T(8,128)(2,1)} %get-tuple-element.48), channel_id=1, source_target_pairs={{0,0},{1,2},{2,32},{3,34},{4,4},{5,6},{6,36},{7,38},{8,8},{9,10},{... | collective-permute-start | bytes 884744 | tf_op jit(solution)/shard_map/ppermute | solution.py:72
  21.8 8.3 %collective-permute-start.9 = (bf16[2,192,384]{2,1,0:T(8,128)(2,1)S(1)}, bf16[2,192,384]{2,1,0:T(8,128)(2,1)S(1)}, u32[]{:S(2)}, u32[]{:S(2)}) collective-permute-start(bf16[2,192,384]{2,1,0:T(8,128)(2,1)S(1)} %get-tuple-element.51), channel_id=1, source_target_pairs={{0,34},{1,32},{2,2},{3,0},{4,38},{5,36},{6,6},{7,4},{8,42},{9,40},... | collective-permute-start | bytes 884744 | tf_op jit(solution)/shard_map/ppermute | solution.py:72
  30.2 0.2 collective-permute-done.5.refs_1_
  30.4 5.1 %collective-permute-start.7 = (bf16[2,192,384]{2,1,0:T(8,128)(2,1)S(1)}, bf16[2,192,384]{2,1,0:T(8,128)(2,1)S(1)}, u32[]{:S(2)}, u32[]{:S(2)}) collective-permute-start(bf16[2,192,384]{2,1,0:T(8,128)(2,1)S(1)} %get-tuple-element.49), channel_id=1, source_target_pairs={{0,2},{1,0},{2,34},{3,32},{4,6},{5,4},{6,38},{7,36},{8,10},{9,8},{... | collective-permute-start | bytes 884744 | tf_op jit(solution)/shard_map/ppermute | solution.py:72
  35.5 3.7 %collective-permute-done.9.refs_3_ = bf16[2,192,384]{2,1,0:T(8,128)(2,1)S(1)} collective-permute-done((bf16[2,192,384]{2,1,0:T(8,128)(2,1)S(1)}, bf16[2,192,384]{2,1,0:T(8,128)(2,1)S(1)}, u32[]{:S(2)}, u32[]{:S(2)}) %collective-permute-start.9) | collective-permute-done | bytes 294944 | tf_op jit(solution)/shard_map/ppermute | solution.py:72
  39.2 0.5 collective-permute-done.8.refs_2_
  39.8 0.2 stack.26
  40.1 0.8 copy-done.6
  40.9 4.3 %collective-permute-start.11 = (bf16[2,768,384]{2,1,0:T(8,128)(2,1)S(1)}, bf16[2,768,384]{2,1,0:T(8,128)(2,1)S(1)}, u32[]{:S(2)}, u32[]{:S(2)}) collective-permute-start(bf16[2,768,384]{2,1,0:T(8,128)(2,1)S(1)} %get-tuple-element.52.refs_2_.refs_1_), channel_id=1, source_target_pairs={{1,64},{3,66},{5,68},{7,70},{9,72},{11,74},{13,76},{15,78},{17,80}... | collective-permute-start | bytes 3538952 | tf_op jit(solution)/shard_map/ppermute | solution.py:72
  45.3 0.6 pad_add_fusion
  45.9 7.0 %collective-permute-start.12 = (bf16[2,384,384]{2,1,0:T(8,128)(2,1)}, bf16[2,384,384]{2,1,0:T(8,128)(2,1)}, u32[]{:S(2)}, u32[]{:S(2)}) collective-permute-start(bf16[2,384,384]{2,1,0:T(8,128)(2,1)} %copy-done.6), channel_id=1, source_target_pairs={{0,16},{1,17},{2,18},{3,19},{4,20},{5,21},{6,22},{7,23},{8,24},{9,... | collective-permute-start | bytes 1769480 | tf_op jit(solution)/shard_map/ppermute | solution.py:72
  52.9 0.7 slice_reduce_fusion
  53.7 0.7 slice_reduce_fusion.1
  54.7 1.0 fusion
  55.9 0.7 fusion.4
  56.7 2.4 %collective-permute-done.11.refs_4_.refs_3_ = bf16[2,768,384]{2,1,0:T(8,128)(2,1)S(1)} collective-permute-done((bf16[2,768,384]{2,1,0:T(8,128)(2,1)S(1)}, bf16[2,768,384]{2,1,0:T(8,128)(2,1)S(1)}, u32[]{:S(2)}, u32[]{:S(2)}) %collective-permute-start.11) | collective-permute-done | bytes 1179680 | tf_op jit(solution)/shard_map/ppermute | solution.py:72
  59.1 1.1 copy-done.1
  60.1 5.7 %attend_2_6.1 = (f32[400,768]{1,0:T(8,128)S(1)}, f32[400,768]{1,0:T(8,128)S(1)}) custom-call(s32[162]{0:T(256)S(1)} %reshape.132.mask_ref, bf16[784,384]{1,0:T(8,128)(2,1)S(1)} %copy-done.1, bf16[784,384]{1,0:T(8,128)(2,1)} %collective-permute-done.5.refs_1_, bf16[2,768,384]{2,1,0:T(8,128)(2,1)S(1)} %get-tuple-element.52.refs_2_.refs_1_, ...), custom_call_target="tpu_custom_call" | custom-call | tf_op jit(solution)/shard_map/attend_2_6/pallas_call | solution.py:309
  65.8 13.3 %collective-permute-done.12.refs_4_.refs_2_ = bf16[2,384,384]{2,1,0:T(8,128)(2,1)} collective-permute-done((bf16[2,384,384]{2,1,0:T(8,128)(2,1)}, bf16[2,384,384]{2,1,0:T(8,128)(2,1)}, u32[]{:S(2)}, u32[]{:S(2)}) %collective-permute-start.12) | collective-permute-done | bytes 589856 | tf_op jit(solution)/shard_map/ppermute | solution.py:72
  79.1 2.0 %collective-permute-start.14 = (bf16[2,384,384]{2,1,0:T(8,128)(2,1)}, bf16[2,384,384]{2,1,0:T(8,128)(2,1)S(1)}, u32[]{:S(2)}, u32[]{:S(2)}) collective-permute-start(bf16[2,384,384]{2,1,0:T(8,128)(2,1)} %collective-permute-done.12.refs_4_.refs_2_), channel_id=1, source_target_pairs={{1,64},{3,66},{5,68},{7,70},{9,72},{11,74},{13,76},{15,78},{17,80}... | collective-permute-start | bytes 1769480 | tf_op jit(solution)/shard_map/ppermute | solution.py:72
  81.2 1.8 %collective-permute-start.13 = (bf16[2,384,384]{2,1,0:T(8,128)(2,1)}, bf16[2,384,384]{2,1,0:T(8,128)(2,1)S(1)}, u32[]{:S(2)}, u32[]{:S(2)}) collective-permute-start(bf16[2,384,384]{2,1,0:T(8,128)(2,1)} %collective-permute-done.12.refs_4_.refs_2_), channel_id=1, source_target_pairs={{0,1},{1,0},{2,3},{3,2},{4,5},{5,4},{6,7},{7,6},{8,9},{9,8},{10,11... | collective-permute-start | bytes 1769480 | tf_op jit(solution)/shard_map/ppermute | solution.py:72
  82.9 7.7 %collective-permute-done.14.refs_6_.refs_4_ = bf16[2,384,384]{2,1,0:T(8,128)(2,1)S(1)} collective-permute-done((bf16[2,384,384]{2,1,0:T(8,128)(2,1)}, bf16[2,384,384]{2,1,0:T(8,128)(2,1)S(1)}, u32[]{:S(2)}, u32[]{:S(2)}) %collective-permute-start.14) | collective-permute-done | bytes 589856 | tf_op jit(solution)/shard_map/ppermute | solution.py:72
  90.6 4.1 %attend_2_3.1 = (bf16[400,768]{1,0:T(8,128)(2,1)S(1)}, bf16[400,768]{1,0:T(8,128)(2,1)S(1)}) custom-call(s32[162]{0:T(256)S(1)} %reshape.132.mask_ref, bf16[784,384]{1,0:T(8,128)(2,1)S(1)} %copy-done.2, bf16[784,384]{1,0:T(8,128)(2,1)} %collective-permute-done.5.refs_1_, bf16[2,384,384]{2,1,0:T(8,128)(2,1)} %collective-permute-done.12.refs_4_.refs_2_, ...), custom_call_target="tpu_custom_call" | custom-call | tf_op jit(solution)/shard_map/attend_2_3/pallas_call | solution.py:309
  94.8 4.7 %collective-permute-start.15 = (bf16[400,768]{1,0:T(8,128)(2,1)S(1)}, bf16[400,768]{1,0:T(8,128)(2,1)S(1)}, u32[]{:S(2)}, u32[]{:S(2)}) collective-permute-start(bf16[400,768]{1,0:T(8,128)(2,1)S(1)} %get-tuple-element.59), channel_id=1, source_target_pairs={{0,4},{1,5},{2,6},{3,7},{4,8},{5,9},{6,10},{7,11},{8,12},{9,13},{1... | collective-permute-start | bytes 1843208 | tf_op jit(solution)/shard_map/ppermute | solution.py:72
  99.5 1.3 collective-permute-start.16
  100.9 9.1 %attend_1_9.1.refs_0_ = f32[400,768]{1,0:T(8,128)S(1)} custom-call(s32[162]{0:T(256)S(1)} %reshape.132.mask_ref, bf16[784,384]{1,0:T(8,128)(2,1)S(1)} %copy-done.4, bf16[2,768,384]{2,1,0:T(8,128)(2,1)S(1)} %get-tuple-element.52.refs_2_.refs_1_, bf16[2,768,384]{2,1,0:T(8,128)(2,1)S(1)} %collective-permute-done.10.refs_3_.refs_2_, ...), custom_call_target="tpu_custom_call" | custom-call | tf_op jit(solution)/shard_map/attend_1_9/pallas_call | solution.py:309
  110.0 2.9 %collective-permute-done.15.refs_1_ = bf16[400,768]{1,0:T(8,128)(2,1)S(1)} collective-permute-done((bf16[400,768]{1,0:T(8,128)(2,1)S(1)}, bf16[400,768]{1,0:T(8,128)(2,1)S(1)}, u32[]{:S(2)}, u32[]{:S(2)}) %collective-permute-start.15) | collective-permute-done | bytes 614432 | tf_op jit(solution)/shard_map/ppermute | solution.py:72
  112.9 4.3 %collective-permute-done.16.refs_2_ = bf16[400,768]{1,0:T(8,128)(2,1)S(1)} collective-permute-done((bf16[400,768]{1,0:T(8,128)(2,1)S(1)}, bf16[400,768]{1,0:T(8,128)(2,1)S(1)}, u32[]{:S(2)}, u32[]{:S(2)}) %collective-permute-start.16) | collective-permute-done | bytes 614432 | tf_op jit(solution)/shard_map/ppermute | solution.py:72
  117.1 1.1 merge.1
  118.2 0.7 collective-permute-start.17
  118.9 3.1 %collective-permute-start.18 = (bf16[192,384]{1,0:T(8,128)(2,1)S(1)}, bf16[192,384]{1,0:T(8,128)(2,1)S(1)}, u32[]{:S(2)}, u32[]{:S(2)}) collective-permute-start(bf16[192,384]{1,0:T(8,128)(2,1)S(1)} %get-tuple-element.62), channel_id=1, source_target_pairs={{2,0},{0,1},{34,2},{32,3},{6,4},{4,5},{38,6},{36,7},{10,8},{8,9},{... | collective-permute-start | bytes 442376 | tf_op jit(solution)/shard_map/ppermute | solution.py:72
  121.9 3.9 %collective-permute-start.20 = (bf16[192,384]{1,0:T(8,128)(2,1)S(1)}, bf16[192,384]{1,0:T(8,128)(2,1)S(1)}, u32[]{:S(2)}, u32[]{:S(2)}) collective-permute-start(bf16[192,384]{1,0:T(8,128)(2,1)S(1)} %get-tuple-element.64), channel_id=1, source_target_pairs={{34,0},{32,1},{2,2},{0,3},{38,4},{36,5},{6,6},{4,7},{42,8},{40,9},... | collective-permute-start | bytes 442376 | tf_op jit(solution)/shard_map/ppermute | solution.py:72
  125.9 1.6 %collective-permute-done.18.refs_1_ = bf16[192,384]{1,0:T(8,128)(2,1)S(1)} collective-permute-done((bf16[192,384]{1,0:T(8,128)(2,1)S(1)}, bf16[192,384]{1,0:T(8,128)(2,1)S(1)}, u32[]{:S(2)}, u32[]{:S(2)}) %collective-permute-start.18) | collective-permute-done | bytes 147488 | tf_op jit(solution)/shard_map/ppermute | solution.py:72
  127.5 2.6 %collective-permute-done.19.refs_2_ = bf16[192,384]{1,0:T(8,128)(2,1)S(1)} collective-permute-done((bf16[192,384]{1,0:T(8,128)(2,1)S(1)}, bf16[192,384]{1,0:T(8,128)(2,1)S(1)}, u32[]{:S(2)}, u32[]{:S(2)}) %collective-permute-start.19) | collective-permute-done | bytes 147488 | tf_op jit(solution)/shard_map/ppermute | solution.py:72
  130.2 4.0 %collective-permute-done.20.refs_3_ = bf16[192,384]{1,0:T(8,128)(2,1)S(1)} collective-permute-done((bf16[192,384]{1,0:T(8,128)(2,1)S(1)}, bf16[192,384]{1,0:T(8,128)(2,1)S(1)}, u32[]{:S(2)}, u32[]{:S(2)}) %collective-permute-start.20) | collective-permute-done | bytes 147488 | tf_op jit(solution)/shard_map/ppermute | solution.py:72
  134.2 0.9 join.1
  (33 shorter events, 1.2 us)
Async XLA Ops:
  0.8 1.5 %copy-start.5 = (bf16[3,192,1536]{2,1,0:T(8,128)(2,1)S(1)}, bf16[3,192,1536]{2,1,0:T(8,128)(2,1)}, u32[]{:S(2)}) copy-start(bf16[3,192,1536]{2,1,0:T(8,128)(2,1)} %qkv_ref.1) | copy-start | bytes 5308420
  3.1 5.9 %collective-permute-start.1 = (bf16[208,384]{1,0:T(8,128)(2,1)S(1)}, bf16[208,384]{1,0:T(8,128)(2,1)S(1)}, u32[]{:S(2)}, u32[]{:S(2)}) collective-permute-start(bf16[208,384]{1,0:T(8,128)(2,1)S(1)} %get-tuple-element.36), channel_id=1, source_target_pairs={{0,2},{1,0},{2,34},{3,32},{4,6},{5,4},{6,38},{7,36},{8,10},{9,8},{... | collective-permute-start | bytes 479240 | tf_op jit(solution)/shard_map/ppermute | solution.py:72
  4.6 7.8 %collective-permute-start.2 = (bf16[208,384]{1,0:T(8,128)(2,1)S(1)}, bf16[208,384]{1,0:T(8,128)(2,1)S(1)}, u32[]{:S(2)}, u32[]{:S(2)}) collective-permute-start(bf16[208,384]{1,0:T(8,128)(2,1)S(1)} %get-tuple-element.39), channel_id=1, source_target_pairs={{0,32},{1,34},{2,0},{3,2},{4,36},{5,38},{6,4},{7,6},{8,40},{9,42},... | collective-permute-start | bytes 479240 | tf_op jit(solution)/shard_map/ppermute | solution.py:72
  6.2 7.3 %collective-permute-start.3 = (bf16[208,384]{1,0:T(8,128)(2,1)S(1)}, bf16[208,384]{1,0:T(8,128)(2,1)S(1)}, u32[]{:S(2)}, u32[]{:S(2)}) collective-permute-start(bf16[208,384]{1,0:T(8,128)(2,1)S(1)} %get-tuple-element.42), channel_id=1, source_target_pairs={{0,34},{1,32},{2,2},{3,0},{4,38},{5,36},{6,6},{7,4},{8,42},{9,40},... | collective-permute-start | bytes 479240 | tf_op jit(solution)/shard_map/ppermute | solution.py:72
  8.4 5.1 %collective-permute-start = (bf16[208,384]{1,0:T(8,128)(2,1)S(1)}, bf16[208,384]{1,0:T(8,128)(2,1)S(1)}, u32[]{:S(2)}, u32[]{:S(2)}) collective-permute-start(bf16[208,384]{1,0:T(8,128)(2,1)S(1)} %get-tuple-element.35), channel_id=1, source_target_pairs={{0,0},{1,2},{2,32},{3,34},{4,4},{5,6},{6,36},{7,38},{8,8},{9,10},{... | collective-permute-start | bytes 479240 | tf_op jit(solution)/shard_map/ppermute | solution.py:72
  14.3 25.4 %copy-start.3 = (bf16[784,384]{1,0:T(8,128)(2,1)}, bf16[784,384]{1,0:T(8,128)(2,1)S(1)}, u32[]{:S(2)}) copy-start(bf16[784,384]{1,0:T(8,128)(2,1)S(1)} %stack_queries.1.refs_0_) | copy-start | bytes 1806340
  14.3 16.1 %collective-permute-start.5 = (bf16[784,384]{1,0:T(8,128)(2,1)S(1)}, bf16[784,384]{1,0:T(8,128)(2,1)}, u32[]{:S(2)}, u32[]{:S(2)}) collective-permute-start(bf16[784,384]{1,0:T(8,128)(2,1)S(1)} %stack_queries.1.refs_0_), channel_id=1, source_target_pairs={{4,0},{5,1},{6,2},{7,3},{8,4},{9,5},{10,6},{11,7},{12,8},{13,9},{1... | collective-permute-start | bytes 1806344 | tf_op jit(solution)/shard_map/ppermute | solution.py:72
  15.6 19.9 %collective-permute-start.4 = (bf16[784,384]{1,0:T(8,128)(2,1)S(1)}, bf16[784,384]{1,0:T(8,128)(2,1)S(1)}, u32[]{:S(2)}, u32[]{:S(2)}) collective-permute-start(bf16[784,384]{1,0:T(8,128)(2,1)S(1)} %stack_queries.1.refs_0_), channel_id=1, source_target_pairs={{0,4},{1,5},{2,6},{3,7},{4,8},{5,9},{6,10},{7,11},{8,12},{9,13},{1... | collective-permute-start | bytes 1806344 | tf_op jit(solution)/shard_map/ppermute | solution.py:72
  20.2 15.3 %collective-permute-start.6 = (bf16[2,192,384]{2,1,0:T(8,128)(2,1)}, bf16[2,192,384]{2,1,0:T(8,128)(2,1)S(1)}, u32[]{:S(2)}, u32[]{:S(2)}) collective-permute-start(bf16[2,192,384]{2,1,0:T(8,128)(2,1)} %get-tuple-element.48), channel_id=1, source_target_pairs={{0,0},{1,2},{2,32},{3,34},{4,4},{5,6},{6,36},{7,38},{8,8},{9,10},{... | collective-permute-start | bytes 884744 | tf_op jit(solution)/shard_map/ppermute | solution.py:72
  21.8 17.4 %collective-permute-start.9 = (bf16[2,192,384]{2,1,0:T(8,128)(2,1)S(1)}, bf16[2,192,384]{2,1,0:T(8,128)(2,1)S(1)}, u32[]{:S(2)}, u32[]{:S(2)}) collective-permute-start(bf16[2,192,384]{2,1,0:T(8,128)(2,1)S(1)} %get-tuple-element.51), channel_id=1, source_target_pairs={{0,34},{1,32},{2,2},{3,0},{4,38},{5,36},{6,6},{7,4},{8,42},{9,40},... | collective-permute-start | bytes 884744 | tf_op jit(solution)/shard_map/ppermute | solution.py:72
  30.1 9.6 %collective-permute-start.8 = (bf16[2,192,384]{2,1,0:T(8,128)(2,1)S(1)}, bf16[2,192,384]{2,1,0:T(8,128)(2,1)S(1)}, u32[]{:S(2)}, u32[]{:S(2)}) collective-permute-start(bf16[2,192,384]{2,1,0:T(8,128)(2,1)S(1)} %get-tuple-element.50), channel_id=1, source_target_pairs={{0,32},{1,34},{2,0},{3,2},{4,36},{5,38},{6,4},{7,6},{8,40},{9,42},... | collective-permute-start | bytes 884744 | tf_op jit(solution)/shard_map/ppermute | solution.py:72
  30.4 9.4 %collective-permute-start.7 = (bf16[2,192,384]{2,1,0:T(8,128)(2,1)S(1)}, bf16[2,192,384]{2,1,0:T(8,128)(2,1)S(1)}, u32[]{:S(2)}, u32[]{:S(2)}) collective-permute-start(bf16[2,192,384]{2,1,0:T(8,128)(2,1)S(1)} %get-tuple-element.49), channel_id=1, source_target_pairs={{0,2},{1,0},{2,34},{3,32},{4,6},{5,4},{6,38},{7,36},{8,10},{9,8},{... | collective-permute-start | bytes 884744 | tf_op jit(solution)/shard_map/ppermute | solution.py:72
  35.5 4.2 %copy-start = (bf16[784,384]{1,0:T(8,128)(2,1)}, bf16[784,384]{1,0:T(8,128)(2,1)S(1)}, u32[]{:S(2)}) copy-start(bf16[784,384]{1,0:T(8,128)(2,1)S(1)} %collective-permute-done.4.refs_0_) | copy-start | bytes 1806340
  40.1 0.8 copy-start.6
  40.9 18.1 %collective-permute-start.11 = (bf16[2,768,384]{2,1,0:T(8,128)(2,1)S(1)}, bf16[2,768,384]{2,1,0:T(8,128)(2,1)S(1)}, u32[]{:S(2)}, u32[]{:S(2)}) collective-permute-start(bf16[2,768,384]{2,1,0:T(8,128)(2,1)S(1)} %get-tuple-element.52.refs_2_.refs_1_), channel_id=1, source_target_pairs={{1,64},{3,66},{5,68},{7,70},{9,72},{11,74},{13,76},{15,78},{17,80}... | collective-permute-start | bytes 3538952 | tf_op jit(solution)/shard_map/ppermute | solution.py:72
  45.2 13.9 %collective-permute-start.10 = (bf16[2,768,384]{2,1,0:T(8,128)(2,1)S(1)}, bf16[2,768,384]{2,1,0:T(8,128)(2,1)S(1)}, u32[]{:S(2)}, u32[]{:S(2)}) collective-permute-start(bf16[2,768,384]{2,1,0:T(8,128)(2,1)S(1)} %get-tuple-element.52.refs_2_.refs_1_), channel_id=1, source_target_pairs={{0,1},{1,0},{2,3},{3,2},{4,5},{5,4},{6,7},{7,6},{8,9},{9,8},{10,11... | collective-permute-start | bytes 3538952 | tf_op jit(solution)/shard_map/ppermute | solution.py:72
  45.9 33.2 %collective-permute-start.12 = (bf16[2,384,384]{2,1,0:T(8,128)(2,1)}, bf16[2,384,384]{2,1,0:T(8,128)(2,1)}, u32[]{:S(2)}, u32[]{:S(2)}) collective-permute-start(bf16[2,384,384]{2,1,0:T(8,128)(2,1)} %copy-done.6), channel_id=1, source_target_pairs={{0,16},{1,17},{2,18},{3,19},{4,20},{5,21},{6,22},{7,23},{8,24},{9,... | collective-permute-start | bytes 1769480 | tf_op jit(solution)/shard_map/ppermute | solution.py:72
  59.1 1.1 copy-start.1
  60.1 30.5 %copy-start.2 = (bf16[784,384]{1,0:T(8,128)(2,1)S(1)}, bf16[784,384]{1,0:T(8,128)(2,1)}, u32[]{:S(2)}) copy-start(bf16[784,384]{1,0:T(8,128)(2,1)} %copy-done) | copy-start | bytes 1806340
  79.1 21.8 %copy-start.4 = (bf16[784,384]{1,0:T(8,128)(2,1)S(1)}, bf16[784,384]{1,0:T(8,128)(2,1)}, u32[]{:S(2)}) copy-start(bf16[784,384]{1,0:T(8,128)(2,1)} %copy-done.3) | copy-start | bytes 1806340
  79.1 11.5 %collective-permute-start.14 = (bf16[2,384,384]{2,1,0:T(8,128)(2,1)}, bf16[2,384,384]{2,1,0:T(8,128)(2,1)S(1)}, u32[]{:S(2)}, u32[]{:S(2)}) collective-permute-start(bf16[2,384,384]{2,1,0:T(8,128)(2,1)} %collective-permute-done.12.refs_4_.refs_2_), channel_id=1, source_target_pairs={{1,64},{3,66},{5,68},{7,70},{9,72},{11,74},{13,76},{15,78},{17,80}... | collective-permute-start | bytes 1769480 | tf_op jit(solution)/shard_map/ppermute | solution.py:72
  81.2 9.5 %collective-permute-start.13 = (bf16[2,384,384]{2,1,0:T(8,128)(2,1)}, bf16[2,384,384]{2,1,0:T(8,128)(2,1)S(1)}, u32[]{:S(2)}, u32[]{:S(2)}) collective-permute-start(bf16[2,384,384]{2,1,0:T(8,128)(2,1)} %collective-permute-done.12.refs_4_.refs_2_), channel_id=1, source_target_pairs={{0,1},{1,0},{2,3},{3,2},{4,5},{5,4},{6,7},{7,6},{8,9},{9,8},{10,11... | collective-permute-start | bytes 1769480 | tf_op jit(solution)/shard_map/ppermute | solution.py:72
  94.8 18.1 %collective-permute-start.15 = (bf16[400,768]{1,0:T(8,128)(2,1)S(1)}, bf16[400,768]{1,0:T(8,128)(2,1)S(1)}, u32[]{:S(2)}, u32[]{:S(2)}) collective-permute-start(bf16[400,768]{1,0:T(8,128)(2,1)S(1)} %get-tuple-element.59), channel_id=1, source_target_pairs={{0,4},{1,5},{2,6},{3,7},{4,8},{5,9},{6,10},{7,11},{8,12},{9,13},{1... | collective-permute-start | bytes 1843208 | tf_op jit(solution)/shard_map/ppermute | solution.py:72
  99.5 17.6 %collective-permute-start.16 = (bf16[400,768]{1,0:T(8,128)(2,1)S(1)}, bf16[400,768]{1,0:T(8,128)(2,1)S(1)}, u32[]{:S(2)}, u32[]{:S(2)}) collective-permute-start(bf16[400,768]{1,0:T(8,128)(2,1)S(1)} %get-tuple-element.60), channel_id=1, source_target_pairs={{4,0},{5,1},{6,2},{7,3},{8,4},{9,5},{10,6},{11,7},{12,8},{13,9},{1... | collective-permute-start | bytes 1843208 | tf_op jit(solution)/shard_map/ppermute | solution.py:72
  118.2 7.7 %collective-permute-start.17 = (bf16[192,384]{1,0:T(8,128)(2,1)S(1)}, bf16[192,384]{1,0:T(8,128)(2,1)S(1)}, u32[]{:S(2)}, u32[]{:S(2)}) collective-permute-start(bf16[192,384]{1,0:T(8,128)(2,1)S(1)} %get-tuple-element.61), channel_id=1, source_target_pairs={{0,0},{2,1},{32,2},{34,3},{4,4},{6,5},{36,6},{38,7},{8,8},{10,9},{... | collective-permute-start | bytes 442376 | tf_op jit(solution)/shard_map/ppermute | solution.py:72
  118.9 8.7 %collective-permute-start.18 = (bf16[192,384]{1,0:T(8,128)(2,1)S(1)}, bf16[192,384]{1,0:T(8,128)(2,1)S(1)}, u32[]{:S(2)}, u32[]{:S(2)}) collective-permute-start(bf16[192,384]{1,0:T(8,128)(2,1)S(1)} %get-tuple-element.62), channel_id=1, source_target_pairs={{2,0},{0,1},{34,2},{32,3},{6,4},{4,5},{38,6},{36,7},{10,8},{8,9},{... | collective-permute-start | bytes 442376 | tf_op jit(solution)/shard_map/ppermute | solution.py:72
  121.9 8.2 %collective-permute-start.19 = (bf16[192,384]{1,0:T(8,128)(2,1)S(1)}, bf16[192,384]{1,0:T(8,128)(2,1)S(1)}, u32[]{:S(2)}, u32[]{:S(2)}) collective-permute-start(bf16[192,384]{1,0:T(8,128)(2,1)S(1)} %get-tuple-element.63), channel_id=1, source_target_pairs={{32,0},{34,1},{0,2},{2,3},{36,4},{38,5},{4,6},{6,7},{40,8},{42,9},... | collective-permute-start | bytes 442376 | tf_op jit(solution)/shard_map/ppermute | solution.py:72
  121.9 12.2 %collective-permute-start.20 = (bf16[192,384]{1,0:T(8,128)(2,1)S(1)}, bf16[192,384]{1,0:T(8,128)(2,1)S(1)}, u32[]{:S(2)}, u32[]{:S(2)}) collective-permute-start(bf16[192,384]{1,0:T(8,128)(2,1)S(1)} %get-tuple-element.64), channel_id=1, source_target_pairs={{34,0},{32,1},{2,2},{0,3},{38,4},{36,5},{6,6},{4,7},{42,8},{40,9},... | collective-permute-start | bytes 442376 | tf_op jit(solution)/shard_map/ppermute | solution.py:72

commit v3 on v2

--- a/solution.py
+++ b/solution.py
@@ -411,6 +411,7 @@
         q_parts[k], kv_pieces[k] = lax.optimization_barrier((q_parts[k], kv_pieces[k]))
     kv_parts = [send(kv_pieces[k], spread_pairs(k)) for k in range(4)]
     q_own = stack_queries(q_parts)
+    q_own, kv_parts[0] = lax.optimization_barrier((q_own, kv_parts[0]))
     q_prev = send(q_own, time_pairs(1))
     q_next = send(q_own, time_pairs(-1))
     place, q_prev, q_next = lax.optimization_barrier((place, q_prev, q_next))

time: 137 us -> 136 us (level); the launches traced: 135 us -> 136 us
  Pallas kernels: 22.7 us -> 26.5 us
  starting transfers between devices: 55.7 us -> 52.9 us
  waiting for transfers between devices: 47.8 us -> 46.2 us
    pallas_call x3, Pallas kernels: 18.9 us -> 22.6 us  [attend(): pl.pallas_call(functools.partial(attend_kernel, sets=sets, pieces=len(sou...]
    ppermute x21, starting transfers between devices: 55.7 us -> 52.9 us  [send(): return lax.ppermute(x, AXES, pairs)]
    ppermute x21, waiting for transfers between devices: 47.8 us -> 46.2 us  [send(): return lax.ppermute(x, AXES, pairs)]
    unnamed x14 -> x20, local copies, waits for them, and re-layouts: 3.37 us -> 4.44 us
  transfers between devices with their start and end apart: 21 -> 21, of which waited for: 14 -> 12; matrix products, arithmetic and copies ran while one was open for 3% -> 3% of each run, Pallas kernels for 11% -> 14%
where the time goes in v3:
time: 136 us
  starting transfers between devices  52.9 us (39%)
  waiting for transfers between devices  46.2 us (34%)
  Pallas kernels  26.5 us (19%)
  local copies, waits for them, and re-layouts  6.46 us (5%)
  other arithmetic  3.28 us (2%)
    ppermute x21, starting transfers between devices, send(): return lax.ppermute(x, AXES, pairs)  52.9 us
    ppermute x21, waiting for transfers between devices, send(): return lax.ppermute(x, AXES, pairs)  46.2 us
    pallas_call x3, Pallas kernels, attend(): pl.pallas_call(functools.partial(attend_kernel, sets=sets, pieces=len(sou...  22.6 us
    unnamed x20, local copies, waits for them, and re-layouts  4.44 us
  transfers between devices with their start and end apart: 21, of which 12 were waited for; matrix products, arithmetic and copies ran while one was open for 3% of the time, Pallas kernels for 14%

profile of v3, /device:TPU:8, one launch (start us, length us, event | category | flops | bytes accessed | tf_op | source)
XLA Modules:
  0.0 135.7 jit_solution(13703885570547941854)
XLA Ops:
  0.0 0.7 convert_element_type.18
  0.8 1.5 %copy-done.8 = bf16[3,192,1536]{2,1,0:T(8,128)(2,1)S(1)} copy-done((bf16[3,192,1536]{2,1,0:T(8,128)(2,1)S(1)}, bf16[3,192,1536]{2,1,0:T(8,128)(2,1)}, u32[]{:S(2)}) %copy-start.8) | copy-done | bytes 1769496
  2.3 1.0 split.1
  3.2 0.7 collective-permute-start.4
  3.9 4.3 %collective-permute-start.1 = (bf16[208,384]{1,0:T(8,128)(2,1)S(1)}, bf16[208,384]{1,0:T(8,128)(2,1)S(1)}, u32[]{:S(2)}, u32[]{:S(2)}) collective-permute-start(bf16[208,384]{1,0:T(8,128)(2,1)S(1)} %get-tuple-element.38), channel_id=1, source_target_pairs={{0,2},{1,0},{2,34},{3,32},{4,6},{5,4},{6,38},{7,36},{8,10},{9,8},{... | collective-permute-start | bytes 479240 | tf_op jit(solution)/shard_map/ppermute | solution.py:72
  8.2 2.4 %collective-permute-start.2 = (bf16[208,384]{1,0:T(8,128)(2,1)S(1)}, bf16[208,384]{1,0:T(8,128)(2,1)S(1)}, u32[]{:S(2)}, u32[]{:S(2)}) collective-permute-start(bf16[208,384]{1,0:T(8,128)(2,1)S(1)} %get-tuple-element.41), channel_id=1, source_target_pairs={{0,32},{1,34},{2,0},{3,2},{4,36},{5,38},{6,4},{7,6},{8,40},{9,42},... | collective-permute-start | bytes 479240 | tf_op jit(solution)/shard_map/ppermute | solution.py:72
  10.6 1.9 %collective-permute-start.3 = (bf16[208,384]{1,0:T(8,128)(2,1)S(1)}, bf16[208,384]{1,0:T(8,128)(2,1)S(1)}, u32[]{:S(2)}, u32[]{:S(2)}) collective-permute-start(bf16[208,384]{1,0:T(8,128)(2,1)S(1)} %get-tuple-element.44), channel_id=1, source_target_pairs={{0,34},{1,32},{2,2},{3,0},{4,38},{5,36},{6,6},{7,4},{8,42},{9,40},... | collective-permute-start | bytes 479240 | tf_op jit(solution)/shard_map/ppermute | solution.py:72
  12.5 0.7 collective-permute-start
  13.2 3.8 %collective-permute-done.2.refs_2_ = bf16[208,384]{1,0:T(8,128)(2,1)S(1)} collective-permute-done((bf16[208,384]{1,0:T(8,128)(2,1)S(1)}, bf16[208,384]{1,0:T(8,128)(2,1)S(1)}, u32[]{:S(2)}, u32[]{:S(2)}) %collective-permute-start.2) | collective-permute-done | bytes 159776 | tf_op jit(solution)/shard_map/ppermute | solution.py:72
  17.1 1.0 collective-permute-done.3.refs_3_
  18.0 0.8 stack_queries.1.refs_0_
  18.9 1.3 collective-permute-start.6
  20.2 4.6 %collective-permute-start.5 = (bf16[784,384]{1,0:T(8,128)(2,1)S(1)}, bf16[784,384]{1,0:T(8,128)(2,1)S(1)}, u32[]{:S(2)}, u32[]{:S(2)}) collective-permute-start(bf16[784,384]{1,0:T(8,128)(2,1)S(1)} %stack_queries.1.refs_0_), channel_id=1, source_target_pairs={{0,4},{1,5},{2,6},{3,7},{4,8},{5,9},{6,10},{7,11},{8,12},{9,13},{1... | collective-permute-start | bytes 1806344 | tf_op jit(solution)/shard_map/ppermute | solution.py:72
  24.8 6.3 %collective-permute-start.9 = (bf16[2,192,384]{2,1,0:T(8,128)(2,1)}, bf16[2,192,384]{2,1,0:T(8,128)(2,1)S(1)}, u32[]{:S(2)}, u32[]{:S(2)}) collective-permute-start(bf16[2,192,384]{2,1,0:T(8,128)(2,1)} %get-tuple-element.55), channel_id=1, source_target_pairs={{0,34},{1,32},{2,2},{3,0},{4,38},{5,36},{6,6},{7,4},{8,42},{9,40},... | collective-permute-start | bytes 884744 | tf_op jit(solution)/shard_map/ppermute | solution.py:72
  31.1 2.0 %collective-permute-start.7 = (bf16[2,192,384]{2,1,0:T(8,128)(2,1)S(1)}, bf16[2,192,384]{2,1,0:T(8,128)(2,1)S(1)}, u32[]{:S(2)}, u32[]{:S(2)}) collective-permute-start(bf16[2,192,384]{2,1,0:T(8,128)(2,1)S(1)} %get-tuple-element.53), channel_id=1, source_target_pairs={{0,2},{1,0},{2,34},{3,32},{4,6},{5,4},{6,38},{7,36},{8,10},{9,8},{... | collective-permute-start | bytes 884744 | tf_op jit(solution)/shard_map/ppermute | solution.py:72
  33.2 2.1 %collective-permute-done.6.refs_1_ = bf16[784,384]{1,0:T(8,128)(2,1)S(1)} collective-permute-done((bf16[784,384]{1,0:T(8,128)(2,1)S(1)}, bf16[784,384]{1,0:T(8,128)(2,1)S(1)}, u32[]{:S(2)}, u32[]{:S(2)}) %collective-permute-start.6) | collective-permute-done | bytes 602144 | tf_op jit(solution)/shard_map/ppermute | solution.py:72
  35.3 1.7 %collective-permute-done.5.refs_0_ = bf16[784,384]{1,0:T(8,128)(2,1)S(1)} collective-permute-done((bf16[784,384]{1,0:T(8,128)(2,1)S(1)}, bf16[784,384]{1,0:T(8,128)(2,1)S(1)}, u32[]{:S(2)}, u32[]{:S(2)}) %collective-permute-start.5) | collective-permute-done | bytes 602144 | tf_op jit(solution)/shard_map/ppermute | solution.py:72
  37.0 4.6 %collective-permute-done.9.refs_3_ = bf16[2,192,384]{2,1,0:T(8,128)(2,1)S(1)} collective-permute-done((bf16[2,192,384]{2,1,0:T(8,128)(2,1)}, bf16[2,192,384]{2,1,0:T(8,128)(2,1)S(1)}, u32[]{:S(2)}, u32[]{:S(2)}) %collective-permute-start.9) | collective-permute-done | bytes 294944 | tf_op jit(solution)/shard_map/ppermute | solution.py:72
  41.9 0.8 copy-done.9
  42.8 2.6 %collective-permute-start.11 = (bf16[2,768,384]{2,1,0:T(8,128)(2,1)S(1)}, bf16[2,768,384]{2,1,0:T(8,128)(2,1)S(1)}, u32[]{:S(2)}, u32[]{:S(2)}) collective-permute-start(bf16[2,768,384]{2,1,0:T(8,128)(2,1)S(1)} %get-tuple-element.56.refs_2_.refs_1_), channel_id=1, source_target_pairs={{1,64},{3,66},{5,68},{7,70},{9,72},{11,74},{13,76},{15,78},{17,80}... | collective-permute-start | bytes 3538952 | tf_op jit(solution)/shard_map/ppermute | solution.py:72
  45.4 1.1 collective-permute-start.10
  47.1 7.0 %collective-permute-start.12 = (bf16[2,384,384]{2,1,0:T(8,128)(2,1)}, bf16[2,384,384]{2,1,0:T(8,128)(2,1)}, u32[]{:S(2)}, u32[]{:S(2)}) collective-permute-start(bf16[2,384,384]{2,1,0:T(8,128)(2,1)} %copy-done.9), channel_id=1, source_target_pairs={{0,16},{1,17},{2,18},{3,19},{4,20},{5,21},{6,22},{7,23},{8,24},{9,... | collective-permute-start | bytes 1769480 | tf_op jit(solution)/shard_map/ppermute | solution.py:72
  54.1 0.7 slice_reduce_fusion.2
  54.9 0.7 slice_reduce_fusion
  55.9 1.0 fusion
  57.1 0.7 fusion.4
  57.9 2.3 %collective-permute-done.11.refs_4_.refs_3_ = bf16[2,768,384]{2,1,0:T(8,128)(2,1)S(1)} collective-permute-done((bf16[2,768,384]{2,1,0:T(8,128)(2,1)S(1)}, bf16[2,768,384]{2,1,0:T(8,128)(2,1)S(1)}, u32[]{:S(2)}, u32[]{:S(2)}) %collective-permute-start.11) | collective-permute-done | bytes 1179680 | tf_op jit(solution)/shard_map/ppermute | solution.py:72
  60.3 1.1 copy-done.1
  61.3 1.1 copy-done.4
  62.4 8.5 %attend_2_6.1 = (f32[400,768]{1,0:T(8,128)S(1)}, f32[400,768]{1,0:T(8,128)S(1)}) custom-call(s32[162]{0:T(256)S(1)} %reshape.132.mask_ref, bf16[784,384]{1,0:T(8,128)(2,1)S(1)} %copy-done.4, bf16[784,384]{1,0:T(8,128)(2,1)S(1)} %copy-done.1, bf16[2,768,384]{2,1,0:T(8,128)(2,1)S(1)} %get-tuple-element.56.refs_2_.refs_1_, ...), custom_call_target="tpu_custom_call" | custom-call | tf_op jit(solution)/shard_map/attend_2_6/pallas_call | solution.py:309
  70.9 8.4 %collective-permute-done.12.refs_4_.refs_2_ = bf16[2,384,384]{2,1,0:T(8,128)(2,1)} collective-permute-done((bf16[2,384,384]{2,1,0:T(8,128)(2,1)}, bf16[2,384,384]{2,1,0:T(8,128)(2,1)}, u32[]{:S(2)}, u32[]{:S(2)}) %collective-permute-start.12) | collective-permute-done | bytes 589856 | tf_op jit(solution)/shard_map/ppermute | solution.py:72
  79.3 2.0 %collective-permute-start.14 = (bf16[2,384,384]{2,1,0:T(8,128)(2,1)}, bf16[2,384,384]{2,1,0:T(8,128)(2,1)S(1)}, u32[]{:S(2)}, u32[]{:S(2)}) collective-permute-start(bf16[2,384,384]{2,1,0:T(8,128)(2,1)} %collective-permute-done.12.refs_4_.refs_2_), channel_id=1, source_target_pairs={{1,64},{3,66},{5,68},{7,70},{9,72},{11,74},{13,76},{15,78},{17,80}... | collective-permute-start | bytes 1769480 | tf_op jit(solution)/shard_map/ppermute | solution.py:72
  81.3 1.5 %collective-permute-start.13 = (bf16[2,384,384]{2,1,0:T(8,128)(2,1)}, bf16[2,384,384]{2,1,0:T(8,128)(2,1)S(1)}, u32[]{:S(2)}, u32[]{:S(2)}) collective-permute-start(bf16[2,384,384]{2,1,0:T(8,128)(2,1)} %collective-permute-done.12.refs_4_.refs_2_), channel_id=1, source_target_pairs={{0,1},{1,0},{2,3},{3,2},{4,5},{5,4},{6,7},{7,6},{8,9},{9,8},{10,11... | collective-permute-start | bytes 1769480 | tf_op jit(solution)/shard_map/ppermute | solution.py:72
  82.8 8.0 %collective-permute-done.14.refs_6_.refs_4_ = bf16[2,384,384]{2,1,0:T(8,128)(2,1)S(1)} collective-permute-done((bf16[2,384,384]{2,1,0:T(8,128)(2,1)}, bf16[2,384,384]{2,1,0:T(8,128)(2,1)S(1)}, u32[]{:S(2)}, u32[]{:S(2)}) %collective-permute-start.14) | collective-permute-done | bytes 589856 | tf_op jit(solution)/shard_map/ppermute | solution.py:72
  90.8 4.1 %attend_2_3.1 = (bf16[400,768]{1,0:T(8,128)(2,1)S(1)}, bf16[400,768]{1,0:T(8,128)(2,1)S(1)}) custom-call(s32[162]{0:T(256)S(1)} %reshape.132.mask_ref, bf16[784,384]{1,0:T(8,128)(2,1)S(1)} %copy-done.5, bf16[784,384]{1,0:T(8,128)(2,1)S(1)} %copy-done.2, bf16[2,384,384]{2,1,0:T(8,128)(2,1)} %collective-permute-done.12.refs_4_.refs_2_, ...), custom_call_target="tpu_custom_call" | custom-call | tf_op jit(solution)/shard_map/attend_2_3/pallas_call | solution.py:309
  94.9 5.0 %collective-permute-start.15 = (bf16[400,768]{1,0:T(8,128)(2,1)S(1)}, bf16[400,768]{1,0:T(8,128)(2,1)S(1)}, u32[]{:S(2)}, u32[]{:S(2)}) collective-permute-start(bf16[400,768]{1,0:T(8,128)(2,1)S(1)} %get-tuple-element.63), channel_id=1, source_target_pairs={{0,4},{1,5},{2,6},{3,7},{4,8},{5,9},{6,10},{7,11},{8,12},{9,13},{1... | collective-permute-start | bytes 1843208 | tf_op jit(solution)/shard_map/ppermute | solution.py:72
  100.0 1.3 collective-permute-start.16
  101.3 10.0 %attend_1_9.1.refs_0_ = f32[400,768]{1,0:T(8,128)S(1)} custom-call(s32[162]{0:T(256)S(1)} %reshape.132.mask_ref, bf16[784,384]{1,0:T(8,128)(2,1)S(1)} %copy-done.7, bf16[2,768,384]{2,1,0:T(8,128)(2,1)S(1)} %get-tuple-element.56.refs_2_.refs_1_, bf16[2,768,384]{2,1,0:T(8,128)(2,1)S(1)} %collective-permute-done.10.refs_3_.refs_2_, ...), custom_call_target="tpu_custom_call" | custom-call | tf_op jit(solution)/shard_map/attend_1_9/pallas_call | solution.py:309
  111.4 1.9 %collective-permute-done.15.refs_1_ = bf16[400,768]{1,0:T(8,128)(2,1)S(1)} collective-permute-done((bf16[400,768]{1,0:T(8,128)(2,1)S(1)}, bf16[400,768]{1,0:T(8,128)(2,1)S(1)}, u32[]{:S(2)}, u32[]{:S(2)}) %collective-permute-start.15) | collective-permute-done | bytes 614432 | tf_op jit(solution)/shard_map/ppermute | solution.py:72
  113.3 4.2 %collective-permute-done.16.refs_2_ = bf16[400,768]{1,0:T(8,128)(2,1)S(1)} collective-permute-done((bf16[400,768]{1,0:T(8,128)(2,1)S(1)}, bf16[400,768]{1,0:T(8,128)(2,1)S(1)}, u32[]{:S(2)}, u32[]{:S(2)}) %collective-permute-start.16) | collective-permute-done | bytes 614432 | tf_op jit(solution)/shard_map/ppermute | solution.py:72
  117.5 1.1 merge.1
  118.5 0.7 collective-permute-start.17
  119.2 1.2 collective-permute-start.18
  120.4 0.9 collective-permute-start.19
  121.3 5.4 %collective-permute-start.20 = (bf16[192,384]{1,0:T(8,128)(2,1)S(1)}, bf16[192,384]{1,0:T(8,128)(2,1)S(1)}, u32[]{:S(2)}, u32[]{:S(2)}) collective-permute-start(bf16[192,384]{1,0:T(8,128)(2,1)S(1)} %get-tuple-element.68), channel_id=1, source_target_pairs={{34,0},{32,1},{2,2},{0,3},{38,4},{36,5},{6,6},{4,7},{42,8},{40,9},... | collective-permute-start | bytes 442376 | tf_op jit(solution)/shard_map/ppermute | solution.py:72
  126.7 0.9 collective-permute-done.19.refs_2_
  127.6 7.2 %collective-permute-done.20.refs_3_ = bf16[192,384]{1,0:T(8,128)(2,1)S(1)} collective-permute-done((bf16[192,384]{1,0:T(8,128)(2,1)S(1)}, bf16[192,384]{1,0:T(8,128)(2,1)S(1)}, u32[]{:S(2)}, u32[]{:S(2)}) %collective-permute-start.20) | collective-permute-done | bytes 147488 | tf_op jit(solution)/shard_map/ppermute | solution.py:72
  134.8 0.9 join.1
  (39 shorter events, 1.9 us)
Async XLA Ops:
  0.8 1.5 %copy-start.8 = (bf16[3,192,1536]{2,1,0:T(8,128)(2,1)S(1)}, bf16[3,192,1536]{2,1,0:T(8,128)(2,1)}, u32[]{:S(2)}) copy-start(bf16[3,192,1536]{2,1,0:T(8,128)(2,1)} %qkv_ref.1) | copy-start | bytes 5308420
  3.2 15.6 %collective-permute-start.4 = (bf16[2,192,384]{2,1,0:T(8,128)(2,1)S(1)}, bf16[2,192,384]{2,1,0:T(8,128)(2,1)S(1)}, u32[]{:S(2)}, u32[]{:S(2)}) collective-permute-start(bf16[2,192,384]{2,1,0:T(8,128)(2,1)S(1)} %get-tuple-element.47), channel_id=1, source_target_pairs={{0,0},{1,2},{2,32},{3,34},{4,4},{5,6},{6,36},{7,38},{8,8},{9,10},{... | collective-permute-start | bytes 884744 | tf_op jit(solution)/shard_map/ppermute | solution.py:72
  3.9 9.3 %collective-permute-start.1 = (bf16[208,384]{1,0:T(8,128)(2,1)S(1)}, bf16[208,384]{1,0:T(8,128)(2,1)S(1)}, u32[]{:S(2)}, u32[]{:S(2)}) collective-permute-start(bf16[208,384]{1,0:T(8,128)(2,1)S(1)} %get-tuple-element.38), channel_id=1, source_target_pairs={{0,2},{1,0},{2,34},{3,32},{4,6},{5,4},{6,38},{7,36},{8,10},{9,8},{... | collective-permute-start | bytes 479240 | tf_op jit(solution)/shard_map/ppermute | solution.py:72
  8.2 8.9 %collective-permute-start.2 = (bf16[208,384]{1,0:T(8,128)(2,1)S(1)}, bf16[208,384]{1,0:T(8,128)(2,1)S(1)}, u32[]{:S(2)}, u32[]{:S(2)}) collective-permute-start(bf16[208,384]{1,0:T(8,128)(2,1)S(1)} %get-tuple-element.41), channel_id=1, source_target_pairs={{0,32},{1,34},{2,0},{3,2},{4,36},{5,38},{6,4},{7,6},{8,40},{9,42},... | collective-permute-start | bytes 479240 | tf_op jit(solution)/shard_map/ppermute | solution.py:72
  10.6 7.4 %collective-permute-start.3 = (bf16[208,384]{1,0:T(8,128)(2,1)S(1)}, bf16[208,384]{1,0:T(8,128)(2,1)S(1)}, u32[]{:S(2)}, u32[]{:S(2)}) collective-permute-start(bf16[208,384]{1,0:T(8,128)(2,1)S(1)} %get-tuple-element.44), channel_id=1, source_target_pairs={{0,34},{1,32},{2,2},{3,0},{4,38},{5,36},{6,6},{7,4},{8,42},{9,40},... | collective-permute-start | bytes 479240 | tf_op jit(solution)/shard_map/ppermute | solution.py:72
  12.5 5.5 %collective-permute-start = (bf16[208,384]{1,0:T(8,128)(2,1)S(1)}, bf16[208,384]{1,0:T(8,128)(2,1)S(1)}, u32[]{:S(2)}, u32[]{:S(2)}) collective-permute-start(bf16[208,384]{1,0:T(8,128)(2,1)S(1)} %get-tuple-element.37), channel_id=1, source_target_pairs={{0,0},{1,2},{2,32},{3,34},{4,4},{5,6},{6,36},{7,38},{8,8},{9,10},{... | collective-permute-start | bytes 479240 | tf_op jit(solution)/shard_map/ppermute | solution.py:72
  18.9 23.1 %copy-start.6 = (bf16[784,384]{1,0:T(8,128)(2,1)}, bf16[784,384]{1,0:T(8,128)(2,1)S(1)}, u32[]{:S(2)}) copy-start(bf16[784,384]{1,0:T(8,128)(2,1)S(1)} %stack_queries.1.refs_0_) | copy-start | bytes 1806340
  18.9 16.4 %collective-permute-start.6 = (bf16[784,384]{1,0:T(8,128)(2,1)S(1)}, bf16[784,384]{1,0:T(8,128)(2,1)S(1)}, u32[]{:S(2)}, u32[]{:S(2)}) collective-permute-start(bf16[784,384]{1,0:T(8,128)(2,1)S(1)} %stack_queries.1.refs_0_), channel_id=1, source_target_pairs={{4,0},{5,1},{6,2},{7,3},{8,4},{9,5},{10,6},{11,7},{12,8},{13,9},{1... | collective-permute-start | bytes 1806344 | tf_op jit(solution)/shard_map/ppermute | solution.py:72
  20.2 16.8 %collective-permute-start.5 = (bf16[784,384]{1,0:T(8,128)(2,1)S(1)}, bf16[784,384]{1,0:T(8,128)(2,1)S(1)}, u32[]{:S(2)}, u32[]{:S(2)}) collective-permute-start(bf16[784,384]{1,0:T(8,128)(2,1)S(1)} %stack_queries.1.refs_0_), channel_id=1, source_target_pairs={{0,4},{1,5},{2,6},{3,7},{4,8},{5,9},{6,10},{7,11},{8,12},{9,13},{1... | collective-permute-start | bytes 1806344 | tf_op jit(solution)/shard_map/ppermute | solution.py:72
  24.8 16.9 %collective-permute-start.9 = (bf16[2,192,384]{2,1,0:T(8,128)(2,1)}, bf16[2,192,384]{2,1,0:T(8,128)(2,1)S(1)}, u32[]{:S(2)}, u32[]{:S(2)}) collective-permute-start(bf16[2,192,384]{2,1,0:T(8,128)(2,1)} %get-tuple-element.55), channel_id=1, source_target_pairs={{0,34},{1,32},{2,2},{3,0},{4,38},{5,36},{6,6},{7,4},{8,42},{9,40},... | collective-permute-start | bytes 884744 | tf_op jit(solution)/shard_map/ppermute | solution.py:72
  31.1 10.6 %collective-permute-start.8 = (bf16[2,192,384]{2,1,0:T(8,128)(2,1)}, bf16[2,192,384]{2,1,0:T(8,128)(2,1)S(1)}, u32[]{:S(2)}, u32[]{:S(2)}) collective-permute-start(bf16[2,192,384]{2,1,0:T(8,128)(2,1)} %get-tuple-element.54), channel_id=1, source_target_pairs={{0,32},{1,34},{2,0},{3,2},{4,36},{5,38},{6,4},{7,6},{8,40},{9,42},... | collective-permute-start | bytes 884744 | tf_op jit(solution)/shard_map/ppermute | solution.py:72
  31.1 10.5 %collective-permute-start.7 = (bf16[2,192,384]{2,1,0:T(8,128)(2,1)S(1)}, bf16[2,192,384]{2,1,0:T(8,128)(2,1)S(1)}, u32[]{:S(2)}, u32[]{:S(2)}) collective-permute-start(bf16[2,192,384]{2,1,0:T(8,128)(2,1)S(1)} %get-tuple-element.53), channel_id=1, source_target_pairs={{0,2},{1,0},{2,34},{3,32},{4,6},{5,4},{6,38},{7,36},{8,10},{9,8},{... | collective-permute-start | bytes 884744 | tf_op jit(solution)/shard_map/ppermute | solution.py:72
  35.3 6.4 %copy-start = (bf16[784,384]{1,0:T(8,128)(2,1)}, bf16[784,384]{1,0:T(8,128)(2,1)S(1)}, u32[]{:S(2)}) copy-start(bf16[784,384]{1,0:T(8,128)(2,1)S(1)} %collective-permute-done.6.refs_1_) | copy-start | bytes 1806340
  37.0 4.7 %copy-start.3 = (bf16[784,384]{1,0:T(8,128)(2,1)}, bf16[784,384]{1,0:T(8,128)(2,1)S(1)}, u32[]{:S(2)}) copy-start(bf16[784,384]{1,0:T(8,128)(2,1)S(1)} %collective-permute-done.5.refs_0_) | copy-start | bytes 1806340
  41.9 0.8 copy-start.9
  42.8 17.5 %collective-permute-start.11 = (bf16[2,768,384]{2,1,0:T(8,128)(2,1)S(1)}, bf16[2,768,384]{2,1,0:T(8,128)(2,1)S(1)}, u32[]{:S(2)}, u32[]{:S(2)}) collective-permute-start(bf16[2,768,384]{2,1,0:T(8,128)(2,1)S(1)} %get-tuple-element.56.refs_2_.refs_1_), channel_id=1, source_target_pairs={{1,64},{3,66},{5,68},{7,70},{9,72},{11,74},{13,76},{15,78},{17,80}... | collective-permute-start | bytes 3538952 | tf_op jit(solution)/shard_map/ppermute | solution.py:72
  45.4 14.9 %collective-permute-start.10 = (bf16[2,768,384]{2,1,0:T(8,128)(2,1)S(1)}, bf16[2,768,384]{2,1,0:T(8,128)(2,1)S(1)}, u32[]{:S(2)}, u32[]{:S(2)}) collective-permute-start(bf16[2,768,384]{2,1,0:T(8,128)(2,1)S(1)} %get-tuple-element.56.refs_2_.refs_1_), channel_id=1, source_target_pairs={{0,1},{1,0},{2,3},{3,2},{4,5},{5,4},{6,7},{7,6},{8,9},{9,8},{10,11... | collective-permute-start | bytes 3538952 | tf_op jit(solution)/shard_map/ppermute | solution.py:72
  47.1 32.2 %collective-permute-start.12 = (bf16[2,384,384]{2,1,0:T(8,128)(2,1)}, bf16[2,384,384]{2,1,0:T(8,128)(2,1)}, u32[]{:S(2)}, u32[]{:S(2)}) collective-permute-start(bf16[2,384,384]{2,1,0:T(8,128)(2,1)} %copy-done.9), channel_id=1, source_target_pairs={{0,16},{1,17},{2,18},{3,19},{4,20},{5,21},{6,22},{7,23},{8,24},{9,... | collective-permute-start | bytes 1769480 | tf_op jit(solution)/shard_map/ppermute | solution.py:72
  60.3 1.1 copy-start.1
  61.3 1.1 copy-start.4
  62.4 28.4 %copy-start.2 = (bf16[784,384]{1,0:T(8,128)(2,1)S(1)}, bf16[784,384]{1,0:T(8,128)(2,1)}, u32[]{:S(2)}) copy-start(bf16[784,384]{1,0:T(8,128)(2,1)} %copy-done) | copy-start | bytes 1806340
  62.4 28.4 %copy-start.5 = (bf16[784,384]{1,0:T(8,128)(2,1)S(1)}, bf16[784,384]{1,0:T(8,128)(2,1)}, u32[]{:S(2)}) copy-start(bf16[784,384]{1,0:T(8,128)(2,1)} %copy-done.3) | copy-start | bytes 1806340
  79.3 22.1 %copy-start.7 = (bf16[784,384]{1,0:T(8,128)(2,1)S(1)}, bf16[784,384]{1,0:T(8,128)(2,1)}, u32[]{:S(2)}) copy-start(bf16[784,384]{1,0:T(8,128)(2,1)} %copy-done.6) | copy-start | bytes 1806340
  79.3 11.5 %collective-permute-start.14 = (bf16[2,384,384]{2,1,0:T(8,128)(2,1)}, bf16[2,384,384]{2,1,0:T(8,128)(2,1)S(1)}, u32[]{:S(2)}, u32[]{:S(2)}) collective-permute-start(bf16[2,384,384]{2,1,0:T(8,128)(2,1)} %collective-permute-done.12.refs_4_.refs_2_), channel_id=1, source_target_pairs={{1,64},{3,66},{5,68},{7,70},{9,72},{11,74},{13,76},{15,78},{17,80}... | collective-permute-start | bytes 1769480 | tf_op jit(solution)/shard_map/ppermute | solution.py:72
  81.3 9.5 %collective-permute-start.13 = (bf16[2,384,384]{2,1,0:T(8,128)(2,1)}, bf16[2,384,384]{2,1,0:T(8,128)(2,1)S(1)}, u32[]{:S(2)}, u32[]{:S(2)}) collective-permute-start(bf16[2,384,384]{2,1,0:T(8,128)(2,1)} %collective-permute-done.12.refs_4_.refs_2_), channel_id=1, source_target_pairs={{0,1},{1,0},{2,3},{3,2},{4,5},{5,4},{6,7},{7,6},{8,9},{9,8},{10,11... | collective-permute-start | bytes 1769480 | tf_op jit(solution)/shard_map/ppermute | solution.py:72
  94.9 18.4 %collective-permute-start.15 = (bf16[400,768]{1,0:T(8,128)(2,1)S(1)}, bf16[400,768]{1,0:T(8,128)(2,1)S(1)}, u32[]{:S(2)}, u32[]{:S(2)}) collective-permute-start(bf16[400,768]{1,0:T(8,128)(2,1)S(1)} %get-tuple-element.63), channel_id=1, source_target_pairs={{0,4},{1,5},{2,6},{3,7},{4,8},{5,9},{6,10},{7,11},{8,12},{9,13},{1... | collective-permute-start | bytes 1843208 | tf_op jit(solution)/shard_map/ppermute | solution.py:72
  100.0 17.5 %collective-permute-start.16 = (bf16[400,768]{1,0:T(8,128)(2,1)S(1)}, bf16[400,768]{1,0:T(8,128)(2,1)S(1)}, u32[]{:S(2)}, u32[]{:S(2)}) collective-permute-start(bf16[400,768]{1,0:T(8,128)(2,1)S(1)} %get-tuple-element.64), channel_id=1, source_target_pairs={{4,0},{5,1},{6,2},{7,3},{8,4},{9,5},{10,6},{11,7},{12,8},{13,9},{1... | collective-permute-start | bytes 1843208 | tf_op jit(solution)/shard_map/ppermute | solution.py:72
  118.5 8.2 %collective-permute-start.17 = (bf16[192,384]{1,0:T(8,128)(2,1)S(1)}, bf16[192,384]{1,0:T(8,128)(2,1)S(1)}, u32[]{:S(2)}, u32[]{:S(2)}) collective-permute-start(bf16[192,384]{1,0:T(8,128)(2,1)S(1)} %get-tuple-element.65), channel_id=1, source_target_pairs={{0,0},{2,1},{32,2},{34,3},{4,4},{6,5},{36,6},{38,7},{8,8},{10,9},{... | collective-permute-start | bytes 442376 | tf_op jit(solution)/shard_map/ppermute | solution.py:72
  119.2 7.5 %collective-permute-start.18 = (bf16[192,384]{1,0:T(8,128)(2,1)S(1)}, bf16[192,384]{1,0:T(8,128)(2,1)S(1)}, u32[]{:S(2)}, u32[]{:S(2)}) collective-permute-start(bf16[192,384]{1,0:T(8,128)(2,1)S(1)} %get-tuple-element.66), channel_id=1, source_target_pairs={{2,0},{0,1},{34,2},{32,3},{6,4},{4,5},{38,6},{36,7},{10,8},{8,9},{... | collective-permute-start | bytes 442376 | tf_op jit(solution)/shard_map/ppermute | solution.py:72
  120.4 7.3 %collective-permute-start.19 = (bf16[192,384]{1,0:T(8,128)(2,1)S(1)}, bf16[192,384]{1,0:T(8,128)(2,1)S(1)}, u32[]{:S(2)}, u32[]{:S(2)}) collective-permute-start(bf16[192,384]{1,0:T(8,128)(2,1)S(1)} %get-tuple-element.67), channel_id=1, source_target_pairs={{32,0},{34,1},{0,2},{2,3},{36,4},{38,5},{4,6},{6,7},{40,8},{42,9},... | collective-permute-start | bytes 442376 | tf_op jit(solution)/shard_map/ppermute | solution.py:72
  121.3 13.5 %collective-permute-start.20 = (bf16[192,384]{1,0:T(8,128)(2,1)S(1)}, bf16[192,384]{1,0:T(8,128)(2,1)S(1)}, u32[]{:S(2)}, u32[]{:S(2)}) collective-permute-start(bf16[192,384]{1,0:T(8,128)(2,1)S(1)} %get-tuple-element.68), channel_id=1, source_target_pairs={{34,0},{32,1},{2,2},{0,3},{38,4},{36,5},{6,6},{4,7},{42,8},{40,9},... | collective-permute-start | bytes 442376 | tf_op jit(solution)/shard_map/ppermute | solution.py:72
